TPU v7x, 32 devices: a whole 2x2x4 slice. The times are simulated.
32 devices in a mesh: dp: 2 (over y), lat: 4 (over x, core), lon: 4 (over z).
Axes of the slice: x: 2, y: 2, z: 4, core: 2. Of those that a mesh axis runs over, the one named last changes fastest.
Arguments:
- fields: bfloat16 [2, 32, 64, 1024], P('dp', 'lat', 'lon'), may hold values from -6 to 6
- cotangent: bfloat16 [2, 32, 64, 512], P('dp', 'lat', 'lon'), may hold values from -6 to 6
- query_weight: bfloat16 [1024, 512], replicated, may hold values from -0.1875 to 0.1875
- keyval_weight: bfloat16 [1024, 1024], replicated, may hold values from -0.1875 to 0.1875
- position_bias: float32 [8, 13, 13], replicated, may hold values from -4 to 4
- land_bias: float32 [8], replicated, may hold values from -2 to 2
- valid_cell: int32 [32, 64], replicated, may hold values 0 or 1
- land_sea: int32 [32, 64], replicated, may hold values 0 or 1
Outputs:
- field_grad: bfloat16 [2, 32, 64, 1024], P('dp', 'lat', 'lon')
- keyval_grad: float32 [1024, 1024], P(('dp', 'lat', 'lon'))
All inputs are finite; a program needn't handle non-finite values.
Results may differ from a plain program's by a relative error of at most 0.011.
Values may be sent and summed in bfloat16 or wider, within the bound.
A program may use at most 128 MiB of HBM per device.

v0:
```python
import jax
import jax.numpy as jnp
from jax import lax
from jax.sharding import PartitionSpec as P

CAP = 20.0


def extended(array, sides, width, wrap):
    for axis, dim in sides:
        size, length = (lax.axis_size(axis), array.shape[dim])
        up = [(i, (i + 1) % size) for i in range(size if wrap else size - 1)]
        down = [(j, i) for i, j in up]
        last = lax.slice_in_dim(array, length - width, length, axis=dim)
        initial = lax.slice_in_dim(array, 0, width, axis=dim)
        before = lax.ppermute(last, axis, up)
        after = lax.ppermute(initial, axis, down)
        array = jnp.concatenate([before, array, after], axis=dim)
    return array


def offset_tables(n_query, n_key, window_side, reach):
    query_idx = jnp.arange(n_query)[:, None]
    key_idx = jnp.arange(n_key)[None, :]
    offset = key_idx - query_idx
    inside = ((offset >= 0) & (offset < window_side)).astype(jnp.float32)
    onehot = (offset[:, :, None] == jnp.arange(window_side)[None, None, :]).astype(jnp.float32)
    centre = (offset == reach).astype(jnp.float32)
    return (inside, onehot, centre)


def score_terms(position_bias, land_bias, land_key, key_ok, row_tab, col_tab, query_ok):
    row_in, row_hot, row_mid = row_tab
    col_in, col_hot, col_mid = col_tab
    partial_bias = jnp.einsum(
        "hab,cxb->hacx", position_bias, col_hot, precision=lax.Precision.HIGHEST
    )
    full_bias = jnp.einsum(
        "hacx,rya->hrcyx", partial_bias, row_hot, precision=lax.Precision.HIGHEST
    )
    n_query = row_hot.shape[0] * col_hot.shape[0]
    n_key = row_hot.shape[1] * col_hot.shape[1]
    full_bias = full_bias.reshape(position_bias.shape[0], n_query, n_key)
    window = row_in[:, None, :, None] * col_in[None, :, None, :]
    centre = row_mid[:, None, :, None] * col_mid[None, :, None, :]
    allowed = window * jnp.maximum(key_ok[None, None], centre) * query_ok[:, :, None, None]
    land_term = land_bias[:, None, None] * land_key.reshape(1, 1, n_key)
    return (full_bias + land_term, allowed.reshape(n_query, n_key))


def window_of(mask, reach, row_start, col_start, n_rows, n_cols):
    floats = mask.astype(jnp.float32)
    padded = jnp.pad(floats, ((reach, reach), (0, 0)))
    wrapped = jnp.concatenate([padded[:, -reach:], padded, padded[:, :reach]], axis=1)
    return lax.dynamic_slice(wrapped, (row_start, col_start), (n_rows, n_cols))


def softmax_grads(query4, key4, value4, dout4, bias, allowed, scale):
    raw = (
        jnp.einsum("qhd,khd->hqk", query4, key4, preferred_element_type=jnp.float32) * scale + bias
    )
    capped = CAP * jnp.tanh(raw / CAP)
    expd = jnp.exp(capped) * allowed[None]
    dots = jnp.einsum("qhd,khd->hqk", dout4, value4, preferred_element_type=jnp.float32)
    denom = jnp.sum(expd, axis=-1, keepdims=True)
    weight = expd / denom
    delta = jnp.sum(weight * dots, axis=-1, keepdims=True)
    weight_b = weight.astype(jnp.bfloat16)
    dscore = (weight * (dots - delta) * (1.0 - (capped / CAP) ** 2) * scale).astype(jnp.bfloat16)
    key_grad = jnp.einsum("hqk,qhd->khd", dscore, query4, preferred_element_type=jnp.float32)
    value_grad = jnp.einsum("hqk,qhd->khd", weight_b, dout4, preferred_element_type=jnp.float32)
    return (dscore, key_grad, value_grad, denom, delta)


def shards(
    fields, cotangent, query_weight, keyval_weight, position_bias, land_bias, valid_cell, land_sea
):
    band_rows, sector_cols, width = (fields.shape[1], fields.shape[2], fields.shape[3])
    q_width = query_weight.shape[1]
    heads_count = position_bias.shape[0]
    head_size = q_width // heads_count
    window_side = position_bias.shape[1]
    reach = (window_side - 1) // 2
    scale = head_size ** (-0.5)
    ext_rows, ext_cols = (band_rows + 2 * reach, sector_cols + 2 * reach)
    n_query = band_rows * sector_cols
    n_key = ext_rows * ext_cols
    flat = fields.reshape(n_query, width)
    queries = jnp.dot(flat, query_weight, preferred_element_type=jnp.float32).astype(jnp.bfloat16)
    keyvals = jnp.dot(flat, keyval_weight, preferred_element_type=jnp.float32).astype(jnp.bfloat16)
    keyvals = keyvals.reshape(band_rows, sector_cols, 2 * q_width)
    keyval_ext = extended(keyvals, (("lat", 0), ("lon", 1)), reach, True)
    row_start = lax.axis_index("lat") * band_rows
    col_start = lax.axis_index("lon") * sector_cols
    key_ok = window_of(valid_cell, reach, row_start, col_start, ext_rows, ext_cols)
    land_key = window_of(land_sea, reach, row_start, col_start, ext_rows, ext_cols)
    row_tab = offset_tables(band_rows, ext_rows, window_side, reach)
    col_tab = offset_tables(sector_cols, ext_cols, window_side, reach)
    own_ok = jnp.ones((band_rows, sector_cols), jnp.float32)
    bias, allowed = score_terms(
        position_bias, land_bias, land_key, key_ok, row_tab, col_tab, own_ok
    )
    query4 = queries.reshape(n_query, heads_count, head_size)
    flat_kv = keyval_ext.reshape(n_key, 2 * q_width)
    key4 = flat_kv[:, :q_width].reshape(n_key, heads_count, head_size)
    value4 = flat_kv[:, q_width:].reshape(n_key, heads_count, head_size)
    dout_flat = cotangent.reshape(n_query, q_width)
    dout4 = dout_flat.reshape(n_query, heads_count, head_size)
    dscore, key_grad, value_grad, denom, delta = softmax_grads(
        query4, key4, value4, dout4, bias, allowed, scale
    )
    query_grad = jnp.einsum("hqk,khd->qhd", dscore, key4, preferred_element_type=jnp.float32)
    query_grad = query_grad.astype(jnp.bfloat16).reshape(n_query, q_width)
    grad_ext = jnp.concatenate(
        [key_grad.reshape(n_key, q_width), value_grad.reshape(n_key, q_width)], axis=-1
    )
    grad_ext = grad_ext.reshape(ext_rows, ext_cols, 2 * q_width)
    side = jnp.concatenate([grad_ext[:, :reach], grad_ext[:, -reach:]], axis=1)
    side_ext = extended(side.astype(jnp.bfloat16), (("lon", 1),), reach, True).astype(side.dtype)
    middle = grad_ext[:, reach:-reach]
    middle = middle.at[:, :reach].add(side_ext[:, :reach])
    middle = middle.at[:, -reach:].add(side_ext[:, -reach:])
    upright = jnp.concatenate([middle[:reach], middle[-reach:]], axis=0)
    upright_ext = extended(upright.astype(jnp.bfloat16), (("lat", 0),), reach, False).astype(
        upright.dtype
    )
    core = middle[reach:-reach]
    core = core.at[:reach].add(upright_ext[:reach])
    core = core.at[-reach:].add(upright_ext[-reach:])
    keyval_cell = core.reshape(n_query, 2 * q_width).astype(jnp.bfloat16)
    contract = (((1,), (1,)), ((), ()))
    field_grad = lax.dot_general(
        query_grad, query_weight, contract, preferred_element_type=jnp.float32
    )
    field_grad = field_grad + lax.dot_general(
        keyval_cell, keyval_weight, contract, preferred_element_type=jnp.float32
    )
    field_grad = field_grad.astype(jnp.bfloat16).reshape(1, band_rows, sector_cols, width)
    members = lax.axis_size("dp")
    grid_devices = lax.axis_size("lat") * lax.axis_size("lon")
    devices_all = members * grid_devices
    norm_factor = float(n_query * devices_all) ** (-0.5)
    term = lax.dot_general(
        flat, keyval_cell, (((0,), (0,)), ((), ())), preferred_element_type=jnp.float32
    )
    keyval_grad = lax.psum_scatter(
        term * norm_factor, ("dp", "lat", "lon"), scatter_dimension=0, tiled=True
    )
    return (field_grad, keyval_grad)


def solution(mesh):
    in_specs = (
        P("dp", "lat", "lon", None),
        P("dp", "lat", "lon", None),
        P(),
        P(),
        P(),
        P(),
        P(),
        P(),
    )
    out_specs = (P("dp", "lat", "lon", None), P(("dp", "lat", "lon"), None))
    return jax.shard_map(shards, mesh=mesh, in_specs=in_specs, out_specs=out_specs, check_vma=False)
```

profile of v0, /device:TPU:0, one launch (start us, length us, event | category | flops | bytes accessed | tf_op | source)
XLA Modules:
  0.0 297.8 jit_solution(8114189008130799533)
XLA Ops:
  7.2 1.5 copy-done
  8.8 1.4 convolution_convert_fusion
  10.2 0.8 fusion.50
  10.9 0.5 collective-permute-start
  11.4 1.9 collective-permute-start.1
  13.6 0.6 iota_subtract_fusion
  14.2 0.1 fusion.20
  14.3 0.7 max.14
  15.0 1.3 broadcast_multiply_fusion.1
  16.3 1.8 mul.119
  18.1 1.4 broadcast_multiply_fusion
  19.5 1.8 mul.123
  21.3 0.6 convolution_bitcast_fusion.3
  21.9 8.0 %convolution_bitcast_fusion = f32[8,8,16,20,28]{4,3,2,0,1:T(8,128)} fusion(f32[8,13,16,28,1]{3,1,2,0,4:T(8,128)S(1)} %convolution_bitcast_fusion.3, s32[8,20]{1,0:T(8,128)S(1)} %iota_subtract_fusion.1), kind=kOutput, calls=%fused_computation.1 | convolution fusion | flops 89458720 | bytes 2480768 | tf_op jit(solution)/shard_map/hacx,rya->hrcyx/dot_general | solution.py:38
  29.9 1.0 convolution_convert_fusion.1
  31.0 0.9 fusion.49
  31.9 2.4 collective-permute-start.2
  34.3 2.0 collective-permute-start.3
  36.4 0.1 copy.37
  36.6 1.7 copy.33
  38.3 10.6 %copy.35 = f32[8,8,16,20,28]{4,3,2,1,0:T(8,128)} copy(f32[8,8,16,20,28]{4,3,2,0,1:T(8,128)} %convolution_bitcast_fusion) | data formatting | bytes 4587520 | tf_op jit(solution)/shard_map/hacx,rya->hrcyx/transpose | solution.py:38
  48.9 9.3 %reshape.321 = f32[8,128,560]{2,1,0:T(8,128)} reshape(f32[8,8,16,20,28]{4,3,2,1,0:T(8,128)} %copy.35) | data formatting | bytes 4587520 | tf_op jit(solution)/shard_map/reshape | solution.py:43
  58.2 3.2 %copy.36 = f32[8,128,560]{1,2,0:T(8,128)} copy(f32[8,128,560]{2,1,0:T(8,128)} %reshape.321) | data formatting | bytes 4587520 | tf_op jit(solution)/shard_map/reshape | solution.py:43
  61.4 0.2 reshape_reshape.3
  61.6 0.8 copy.39
  62.5 2.8 pad_maximum_fusion
  65.3 1.4 reshape.318
  66.8 1.1 fusion.47
  67.8 1.4 copy.50
  69.2 3.2 %fusion.6 = (f32[8,128]{1,0:T(8,128)S(1)}, f32[8,128,560]{1,2,0:T(8,128)S(1)}) fusion(f32[128,560]{0,1:T(8,128)S(1)} %copy.37, f32[8,128,560]{1,2,0:T(8,128)} %copy.36, f32[8,560]{1,0:T(8,128)S(1)} %broadcast_multiply_fusion.2, bf16[128,8,64]{0,2,1:T(8,128)(2,1)} %bitcast.86, bf16[560,8,64]{0,2,1:T(8,128)(2,1)S(1)} %bitcast.79), kind=kOutput, calls=%fused_computation.12 | convolution fusion | flops 77413376 | bytes 5600768 | tf_op jit(solution)/shard_map/qhd,khd->hqk/dot_general | solution.py:60
  72.4 1.4 copy-done.9
  73.9 1.6 convolution_bitcast_fusion.1
  75.5 2.0 copy.42
  77.5 2.0 concatenate.45
  79.5 2.1 copy.51
  81.7 3.1 %fusion.51 = f32[8,560,128]{2,1,0:T(8,128)} fusion(bf16[560,8,64]{0,2,1:T(8,128)(2,1)} %bitcast.78, bf16[128,8,64]{0,2,1:T(8,128)(2,1)S(1)} %copy-done.18), kind=kOutput, calls=%fused_computation.89 | convolution fusion | flops 73400320 | bytes 2998272 | tf_op jit(solution)/shard_map/qhd,khd->hqk/dot_general | solution.py:64
  84.8 6.4 %convolution_bitcast_fusion.2 = f32[560,8,64]{0,2,1:T(8,128)} fusion(bf16[128,8,64]{0,2,1:T(8,128)(2,1)} %bitcast.87, f32[8,560,128]{2,1,0:T(8,128)} %fusion.51, f32[8,128,560]{1,2,0:T(8,128)} %copy-done.9, f32[8,128]{1,0:T(8,128)S(1)} %get-tuple-element.70, f32[128,560]{0,1:T(8,128)} %copy-done.12), kind=kOutput, calls=%fused_computation.14 | convolution fusion | flops 81430064 | bytes 6156288 | tf_op jit(solution)/shard_map/hqk,qhd->khd/dot_general | solution.py:70
  91.2 3.0 %copy.40 = f32[560,8,64]{2,1,0:T(8,128)} copy(f32[560,8,64]{0,2,1:T(8,128)} %convolution_bitcast_fusion.2) | data formatting | bytes 2293760 | tf_op jit(solution)/shard_map/hqk,qhd->khd/transpose | solution.py:70
  94.2 2.8 concatenate.44
  97.0 1.4 constant_dynamic-update-slice_fusion.1
  98.4 0.1 constant_dynamic-update-slice_fusion
  98.5 0.2 convert.12
  98.7 0.1 fusion.46
  98.9 3.8 %collective-permute-start.5 = (bf16[20,6,1024]{2,1,0:T(8,128)(2,1)S(1)}, bf16[20,6,1024]{2,1,0:T(8,128)(2,1)S(1)}, u32[]{:S(2)}, u32[]{:S(2)}) collective-permute-start(bf16[20,6,1024]{2,1,0:T(8,128)(2,1)S(1)} %get-tuple-element.57), channel_id=1, source_target_pairs={{1,0},{2,1},{3,2},{0,3},{5,4},{6,5},{7,6},{4,7},{9,8},{10,9},{11,1... | collective-permute-start | bytes 737288 | tf_op jit(solution)/shard_map/ppermute | solution.py:17
  102.7 0.2 slice.204
  102.9 8.4 %collective-permute-done.4 = bf16[20,6,1024]{2,1,0:T(8,128)(2,1)S(1)} collective-permute-done((bf16[20,6,1024]{2,1,0:T(8,128)(2,1)S(1)}, bf16[20,6,1024]{2,1,0:T(8,128)(2,1)S(1)}, u32[]{:S(2)}, u32[]{:S(2)}) %collective-permute-start.4) | collective-permute-done | bytes 245792 | tf_op jit(solution)/shard_map/ppermute | solution.py:16
  111.4 3.9 %collective-permute-done.5 = bf16[20,6,1024]{2,1,0:T(8,128)(2,1)S(1)} collective-permute-done((bf16[20,6,1024]{2,1,0:T(8,128)(2,1)S(1)}, bf16[20,6,1024]{2,1,0:T(8,128)(2,1)S(1)}, u32[]{:S(2)}, u32[]{:S(2)}) %collective-permute-start.5) | collective-permute-done | bytes 245792 | tf_op jit(solution)/shard_map/ppermute | solution.py:17
  115.2 0.7 copy-done.11
  116.0 1.1 convert_add_fusion
  117.1 3.5 %scatter-add.14 = f32[20,16,1024]{2,1,0:T(8,128)S(1)} dynamic-update-slice(f32[20,16,1024]{2,1,0:T(8,128)S(1)} %slice.204, f32[20,6,1024]{2,1,0:T(8,128)} %convert_add_fusion, s32[]{:T(128)} %constant.135.clone.1, s32[]{:T(128)} %constant.135.clone.1, s32[]{:T(128)} %constant.135.clone.1) | dynamic-update-slice | bytes 983044 | tf_op jit(solution)/shard_map/scatter-add | solution.py:121
  120.6 2.1 slice_add_fusion
  122.7 3.4 %scatter-add.15 = f32[20,16,1024]{2,1,0:T(8,128)S(1)} dynamic-update-slice(f32[20,16,1024]{2,1,0:T(8,128)S(1)} %scatter-add.14, f32[20,6,1024]{2,1,0:T(8,128)} %slice_add_fusion, s32[]{:T(128)} %constant.135.clone.1, s32[]{:T(128)} %constant.144.clone.1, s32[]{:T(128)} %constant.135.clone.1) | dynamic-update-slice | bytes 983044 | tf_op jit(solution)/shard_map/scatter-add | solution.py:122
  126.2 0.1 convert.13
  126.3 1.3 collective-permute-start.6
  127.7 1.6 collective-permute-start.7
  129.4 2.5 collective-permute-done.7
  132.1 2.8 multiply_bitcast_fusion
  134.9 5.3 %copy.48 = f32[1024,1024]{1,0:T(8,128)} copy(f32[1024,1024]{0,1:T(8,128)} %multiply_bitcast_fusion) | data formatting | bytes 8388608
  140.2 1.1 copy-done.6
  141.3 5.5 %convolution_convert_fusion.2 = bf16[8,64,128]{2,1,0:T(8,128)(2,1)S(1)} fusion(bf16[560,8,64]{0,2,1:T(8,128)(2,1)S(1)} %bitcast.80, f32[8,560,128]{2,1,0:T(8,128)} %fusion.51, f32[8,128,560]{1,2,0:T(8,128)} %copy-done.9, f32[8,128]{1,0:T(8,128)S(1)} %get-tuple-element.70, f32[128,560]{0,1:T(8,128)} %copy-done.12), kind=kOutput, calls=%fused_computation.21 | convolution fusion | flops 81495600 | bytes 5582848 | tf_op jit(solution)/shard_map/hqk,khd->qhd/dot_general | solution.py:112
  146.8 0.8 fusion.52
  147.6 0.4 copy-done.2
  148.0 1.2 fusion.7
  149.2 141.7 %reduce-scatter.4.cloned.1.call-done = f32[32,1024]{1,0:T(8,128)} async-done(((f32[1024,1024]{1,0:T(8,128)}), f32[32,1024]{1,0:T(8,128)}) %reduce-scatter.4.cloned.1.call-update) | async-done | bytes 131088
  (75 shorter events, 1.0 us)
Async XLA Ops:
  7.2 1.6 copy-start
  7.2 6.2 %copy-start.23 = (s32[32,64]{1,0:T(8,128)S(1)}, s32[32,64]{1,0:T(8,128)}, u32[]{:S(2)}) copy-start(s32[32,64]{1,0:T(8,128)} %param.22) | copy-start | bytes 24580
  7.2 6.2 %copy-start.24 = (s32[32,64]{1,0:T(8,128)S(1)}, s32[32,64]{1,0:T(8,128)}, u32[]{:S(2)}) copy-start(s32[32,64]{1,0:T(8,128)} %param.23) | copy-start | bytes 24580
  7.2 283.8 %reduce-scatter.4.cloned.1.call-start = ((), (), s32[]{:S(2)}) async-start(), calls=%async_computation.1 | async-start | bytes 4325376
  10.9 19.9 %collective-permute-start = (bf16[6,16,1024]{2,1,0:T(8,128)(2,1)}, bf16[6,16,1024]{2,1,0:T(8,128)(2,1)S(1)}, u32[]{:S(2)}, u32[]{:S(2)}) collective-permute-start(bf16[6,16,1024]{2,1,0:T(8,128)(2,1)} %bitcast.1), channel_id=1, source_target_pairs={{0,4},{4,8},{8,12},{12,0},{1,5},{5,9},{9,13},{13,1},{2,6},{6,10},{... | collective-permute-start | bytes 589832 | tf_op jit(solution)/shard_map/ppermute | solution.py:16
  11.4 19.5 %collective-permute-start.1 = (bf16[6,16,1024]{2,1,0:T(8,128)(2,1)}, bf16[6,16,1024]{2,1,0:T(8,128)(2,1)S(1)}, u32[]{:S(2)}, u32[]{:S(2)}) collective-permute-start(bf16[6,16,1024]{2,1,0:T(8,128)(2,1)} %bitcast.3), channel_id=1, source_target_pairs={{4,0},{8,4},{12,8},{0,12},{5,1},{9,5},{13,9},{1,13},{6,2},{10,6},{... | collective-permute-start | bytes 589832 | tf_op jit(solution)/shard_map/ppermute | solution.py:17
  16.3 5.0 %copy-start.20 = (f32[8,13,13]{2,0,1:T(8,128)S(1)}, f32[8,13,13]{2,0,1:T(8,128)}, u32[]{:S(2)}) copy-start(f32[8,13,13]{2,0,1:T(8,128)} %param.20) | copy-start | bytes 16228
  16.3 5.0 %copy-start.21 = (s32[16,28]{1,0:T(8,128)S(1)}, s32[16,28]{1,0:T(8,128)}, u32[]{:S(2)}) copy-start(s32[16,28]{1,0:T(8,128)} %iota_subtract_fusion) | copy-start | bytes 5380
  21.9 8.0 %copy-start.1 = (bf16[1024,512]{1,0:T(8,128)(2,1)S(1)}, bf16[1024,512]{1,0:T(8,128)(2,1)}, u32[]{:S(2)}) copy-start(bf16[1024,512]{1,0:T(8,128)(2,1)} %param.18) | copy-start | bytes 3145732
  21.9 8.0 %copy-start.7 = (bf16[1,8,16,1024]{3,2,1,0:T(8,128)(2,1)S(1)}, bf16[1,8,16,1024]{3,2,1,0:T(8,128)(2,1)}, u32[]{:S(2)}) copy-start(bf16[1,8,16,1024]{3,2,1,0:T(8,128)(2,1)} %param.16) | copy-start | bytes 786436
  29.9 6.5 %copy-start.22 = (f32[560]{0:T(1024)S(1)}, f32[560]{0:T(1024)}, u32[]{:S(2)}) copy-start(f32[560]{0:T(1024)} %max.14) | copy-start | bytes 6724
  30.9 3.4 %copy-start.13 = (bf16[6,16,1024]{2,1,0:T(8,128)(2,1)}, bf16[6,16,1024]{2,1,0:T(8,128)(2,1)S(1)}, u32[]{:S(2)}) copy-start(bf16[6,16,1024]{2,1,0:T(8,128)(2,1)S(1)} %collective-permute-done) | copy-start | bytes 589828
  30.9 5.5 %copy-start.15 = (bf16[6,16,1024]{2,1,0:T(8,128)(2,1)}, bf16[6,16,1024]{2,1,0:T(8,128)(2,1)S(1)}, u32[]{:S(2)}) copy-start(bf16[6,16,1024]{2,1,0:T(8,128)(2,1)S(1)} %collective-permute-done.1) | copy-start | bytes 589828
  31.9 30.6 %collective-permute-start.2 = (bf16[20,6,1024]{2,1,0:T(8,128)(2,1)}, bf16[20,6,1024]{2,1,0:T(8,128)(2,1)}, u32[]{:S(2)}, u32[]{:S(2)}) collective-permute-start(bf16[20,6,1024]{2,1,0:T(8,128)(2,1)} %get-tuple-element.62), channel_id=1, source_target_pairs={{0,1},{1,2},{2,3},{3,0},{4,5},{5,6},{6,7},{7,4},{8,9},{9,10},{10,1... | collective-permute-start | bytes 737288 | tf_op jit(solution)/shard_map/ppermute | solution.py:16
  34.3 28.2 %collective-permute-start.3 = (bf16[20,6,1024]{2,1,0:T(8,128)(2,1)}, bf16[20,6,1024]{2,1,0:T(8,128)(2,1)}, u32[]{:S(2)}, u32[]{:S(2)}) collective-permute-start(bf16[20,6,1024]{2,1,0:T(8,128)(2,1)} %get-tuple-element.63), channel_id=1, source_target_pairs={{1,0},{2,1},{3,2},{0,3},{5,4},{6,5},{7,6},{4,7},{9,8},{10,9},{11,1... | collective-permute-start | bytes 737288 | tf_op jit(solution)/shard_map/ppermute | solution.py:17
  36.5 32.7 %copy-start.12 = (f32[128,560]{0,1:T(8,128)}, f32[128,560]{0,1:T(8,128)S(1)}, u32[]{:S(2)}) copy-start(f32[128,560]{0,1:T(8,128)S(1)} %copy.37) | copy-start | bytes 860164
  58.2 3.2 %copy-start.19 = (bf16[1,8,16,512]{3,2,1,0:T(8,128)(2,1)S(1)}, bf16[1,8,16,512]{3,2,1,0:T(8,128)(2,1)}, u32[]{:S(2)}) copy-start(bf16[1,8,16,512]{3,2,1,0:T(8,128)(2,1)} %param.17) | copy-start | bytes 393220
  58.2 4.3 %copy-start.25 = (f32[8]{0:T(128)S(1)}, f32[8]{0:T(128)}, u32[]{:S(2)}) copy-start(f32[8]{0:T(128)} %param.21) | copy-start | bytes 100
  58.2 4.3 %copy-start.14 = (bf16[6,16,1024]{2,1,0:T(8,128)(2,1)S(1)}, bf16[6,16,1024]{2,1,0:T(8,128)(2,1)}, u32[]{:S(2)}) copy-start(bf16[6,16,1024]{2,1,0:T(8,128)(2,1)} %copy-done.13) | copy-start | bytes 589828
  58.2 4.3 %copy-start.16 = (bf16[6,16,1024]{2,1,0:T(8,128)(2,1)S(1)}, bf16[6,16,1024]{2,1,0:T(8,128)(2,1)}, u32[]{:S(2)}) copy-start(bf16[6,16,1024]{2,1,0:T(8,128)(2,1)} %copy-done.15) | copy-start | bytes 589828
  69.2 3.2 %copy-start.5 = (bf16[560,512]{0,1:T(8,128)(2,1)}, bf16[560,512]{0,1:T(8,128)(2,1)S(1)}, u32[]{:S(2)}) copy-start(bf16[560,512]{0,1:T(8,128)(2,1)S(1)} %copy.50) | copy-start | bytes 1720324
  69.2 4.6 %copy-start.17 = (bf16[128,8,64]{0,2,1:T(8,128)(2,1)S(1)}, bf16[128,8,64]{0,2,1:T(8,128)(2,1)}, u32[]{:S(2)}) copy-start(bf16[128,8,64]{0,2,1:T(8,128)(2,1)} %copy.39) | copy-start | bytes 393220
  72.4 1.4 copy-start.9
  77.5 4.1 %copy-start.18 = (bf16[128,8,64]{0,2,1:T(8,128)(2,1)S(1)}, bf16[128,8,64]{0,2,1:T(8,128)(2,1)}, u32[]{:S(2)}) copy-start(bf16[128,8,64]{0,2,1:T(8,128)(2,1)} %copy.39) | copy-start | bytes 393220
  98.9 16.4 %copy-start.3 = (bf16[20,6,1024]{2,1,0:T(8,128)(2,1)}, bf16[20,6,1024]{2,1,0:T(8,128)(2,1)S(1)}, u32[]{:S(2)}) copy-start(bf16[20,6,1024]{2,1,0:T(8,128)(2,1)S(1)} %get-tuple-element.56) | copy-start | bytes 737284
  98.9 16.4 %copy-start.4 = (bf16[20,6,1024]{2,1,0:T(8,128)(2,1)}, bf16[20,6,1024]{2,1,0:T(8,128)(2,1)S(1)}, u32[]{:S(2)}) copy-start(bf16[20,6,1024]{2,1,0:T(8,128)(2,1)S(1)} %get-tuple-element.57) | copy-start | bytes 737284
  98.9 12.5 %collective-permute-start.4 = (bf16[20,6,1024]{2,1,0:T(8,128)(2,1)S(1)}, bf16[20,6,1024]{2,1,0:T(8,128)(2,1)S(1)}, u32[]{:S(2)}, u32[]{:S(2)}) collective-permute-start(bf16[20,6,1024]{2,1,0:T(8,128)(2,1)S(1)} %get-tuple-element.56), channel_id=1, source_target_pairs={{0,1},{1,2},{2,3},{3,0},{4,5},{5,6},{6,7},{7,4},{8,9},{9,10},{10,1... | collective-permute-start | bytes 737288 | tf_op jit(solution)/shard_map/ppermute | solution.py:16
  98.9 16.3 %collective-permute-start.5 = (bf16[20,6,1024]{2,1,0:T(8,128)(2,1)S(1)}, bf16[20,6,1024]{2,1,0:T(8,128)(2,1)S(1)}, u32[]{:S(2)}, u32[]{:S(2)}) collective-permute-start(bf16[20,6,1024]{2,1,0:T(8,128)(2,1)S(1)} %get-tuple-element.57), channel_id=1, source_target_pairs={{1,0},{2,1},{3,2},{0,3},{5,4},{6,5},{7,6},{4,7},{9,8},{10,9},{11,1... | collective-permute-start | bytes 737288 | tf_op jit(solution)/shard_map/ppermute | solution.py:17
  111.4 3.9 %copy-start.10 = (bf16[20,6,1024]{2,1,0:T(8,128)(2,1)}, bf16[20,6,1024]{2,1,0:T(8,128)(2,1)S(1)}, u32[]{:S(2)}) copy-start(bf16[20,6,1024]{2,1,0:T(8,128)(2,1)S(1)} %collective-permute-done.4) | copy-start | bytes 737284
  115.2 0.7 copy-start.11
  126.3 3.0 %collective-permute-start.6 = (bf16[6,16,1024]{2,1,0:T(8,128)(2,1)S(1)}, bf16[6,16,1024]{2,1,0:T(8,128)(2,1)S(1)}, u32[]{:S(2)}, u32[]{:S(2)}) collective-permute-start(bf16[6,16,1024]{2,1,0:T(8,128)(2,1)S(1)} %get-tuple-element.60), channel_id=1, source_target_pairs={{0,4},{4,8},{8,12},{1,5},{5,9},{9,13},{2,6},{6,10},{10,14},{3,7},{... | collective-permute-start | bytes 589832 | tf_op jit(solution)/shard_map/ppermute | solution.py:16
  127.6 4.4 %copy-start.8 = (bf16[1,8,16,1024]{3,2,1,0:T(8,128)(2,1)S(1)}, bf16[1,8,16,1024]{3,2,1,0:T(8,128)(2,1)}, u32[]{:S(2)}) copy-start(bf16[1,8,16,1024]{3,2,1,0:T(8,128)(2,1)} %param.16) | copy-start | bytes 786436
  127.7 4.2 %collective-permute-start.7 = (bf16[6,16,1024]{2,1,0:T(8,128)(2,1)S(1)}, bf16[6,16,1024]{2,1,0:T(8,128)(2,1)S(1)}, u32[]{:S(2)}, u32[]{:S(2)}) collective-permute-start(bf16[6,16,1024]{2,1,0:T(8,128)(2,1)S(1)} %get-tuple-element.61), channel_id=1, source_target_pairs={{4,0},{8,4},{12,8},{5,1},{9,5},{13,9},{6,2},{10,6},{14,10},{7,3},{... | collective-permute-start | bytes 589832 | tf_op jit(solution)/shard_map/ppermute | solution.py:17
  140.2 1.1 copy-start.6
  146.8 1.2 copy-start.2
Sparse Core Ops, SparseCore 0:
  140.3 150.5 reduce-scatter.3
where the time goes:
time: 299 us; the launch traced here: 298 us
  waiting for transfers between devices  157 us (53%)
  local copies, waits for them, and re-layouts  67.4 us (23%)
  matrix products  35.5 us (12%)
  between operations  14.5 us (5%)
  starting transfers between devices  13.7 us (5%)
  other arithmetic  10.1 us (3%)
    unnamed x2, waiting for transfers between devices  142 us
    unnamed x56, local copies, waits for them, and re-layouts  15.5 us
    reshape x2, local copies, waits for them, and re-layouts, score_terms(): full_bias = full_bias.reshape(position_bias.shape[0], n_query, n_key)  12.5 us
    transpose x1, local copies, waits for them, and re-layouts, score_terms(): jnp.einsum('hacx,rya->hrcyx', partial_bias, row_hot, precision=lax.Precis...  10.6 us
    ppermute x4, starting transfers between devices, extended(): after = lax.ppermute(initial, axis, down)  9.42 us
    ppermute x4, waiting for transfers between devices, extended(): before = lax.ppermute(last, axis, up)  8.45 us
    dot_general x1, matrix products, score_terms(): jnp.einsum('hacx,rya->hrcyx', partial_bias, row_hot, precision=lax.Precis...  7.98 us
    dot_general x1, matrix products, softmax_grads(): jnp.einsum('hqk,qhd->khd', dscore, query4, preferred_element_type=jnp.flo...  6.39 us
  transfers between devices with their start and end apart: 9, of which 4 were waited for; matrix products, arithmetic and copies ran while one was open for 17% of the time, Pallas kernels for 0%

commit v1 on v0

v1 whole, which is shorter than its diff:
```python
import jax
import jax.numpy as jnp
from jax import lax
from jax.experimental import pallas as pl
from jax.experimental.pallas import tpu as pltpu
from jax.sharding import PartitionSpec as P

CAP = 20.0
MESH = pl.DeviceIdType.MESH
F32, BF16 = jnp.float32, jnp.bfloat16
OCT = 8
NEAR = (((1,), (1,)), ((), ()))
TALL = (((0,), (0,)), ((), ()))


class Plan:
    def __init__(self, rows, cols, reach, heads, size, lat, lon, dp):
        self.rows, self.cols, self.reach, self.heads, self.size = rows, cols, reach, heads, size
        self.lat, self.lon, self.dp = lat, lon, dp
        self.nq = rows * cols
        self.ext = rows + 2 * reach
        self.octets = cols // OCT + 2
        self.per_oct = self.ext * OCT
        self.nk = self.octets * self.per_oct
        self.half = rows * OCT
        self.groups = heads // 2
        self.edge = reach * OCT
        self.regions = []
        last = self.octets - 1
        for o in range(self.octets):
            for part in (-1, 0, 1):
                step = -1 if o == 0 else (1 if o == last else 0)
                if step == 0 and part == 0:
                    continue
                owner = last - 1 if o == 0 else (1 if o == last else o)
                start = (self.half - self.edge) if part == -1 else 0
                count = self.half if part == 0 else self.edge
                at = o * self.per_oct + (0 if part == -1 else self.edge + (0 if part == 0 else self.half))
                self.regions.append((step, part, owner, start, count, at))
        self.group_all = dp == 2 and lat == 4

    def own_at(self, o):
        return o * self.per_oct + self.edge


def body(pn, scale, norm, refs):
    (f_ref, d_ref, wq_ref, wkv_ref, lines_ref, land_bias_ref, valid_ref, land_ref) = refs[:8]
    if pn.group_all:
        fg_out, kv_out = refs[8:10]
        rest = refs[10:]
    else:
        fg_out, cell_out = refs[8:10]
        rest = refs[10:]
    (ext, gsend, grecv, own, q2, do2, bias, okay, dq_s, hs, hr, gs, gr) = rest[:13]
    if pn.group_all:
        (fall, cell, kall, zsend, zrecv, fsum, ocol, fs, fr, ks, kr, zs, zr, os_, or_) = rest[13:]
    lat, lon, dp = lax.axis_index("lat"), lax.axis_index("lon"), lax.axis_index("dp")
    nlat, nlon = pn.lat, pn.lon
    hd = pn.size
    gw = 2 * hd
    qw = pn.heads * hd

    def at(dlat, dlon, ddp=0):
        return (
            lax.rem(dp + ddp, pn.dp) if ddp else dp,
            lax.rem(lat + dlat + nlat, nlat) if dlat else lat,
            lax.rem(lon + dlon + nlon, nlon) if dlon else lon,
        )

    peers = [(0, a, b) for a in (-1, 0, 1) for b in (-1, 0, 1) if a or b]
    if pn.group_all:
        steps = [(d, a, 0) for d in range(2) for a in range(-1, 3) if d or a]
        steps += [(0, 0, b) for b in range(1, nlon)]
        for d, a, b in steps:
            seen = {(u, v % nlat, w % nlon) for u, v, w in peers}
            if (d, a % nlat, b % nlon) not in seen:
                peers.append((d, a, b))
    barrier = pltpu.get_barrier_semaphore()
    for d, a, b in peers:
        pl.semaphore_signal(barrier, inc=1, device_id=at(a, b, d), device_id_type=MESH)
    pl.semaphore_wait(barrier, len(peers))

    def remote(src, dst, ssem, rsem, dev):
        return pltpu.make_async_remote_copy(
            src_ref=src, dst_ref=dst, send_sem=ssem, recv_sem=rsem, device_id=dev, device_id_type=MESH
        )

    def halo(g, i):
        step, part, owner, start, count, where = pn.regions[i]
        return remote(
            ext.at[g, pl.ds(pn.own_at(owner) + start, count)],
            ext.at[g, pl.ds(where, count)],
            hs.at[g, i], hr.at[g, i], at(-part, -step),
        )

    def back(g, i):
        step, part, owner, start, count, where = pn.regions[i]
        return remote(
            gsend.at[g, pl.ds(where, count)],
            grecv.at[g, pl.ds(where, count)],
            gs.at[g, i], gr.at[g, i], at(part, step),
        )

    nreg = len(pn.regions)

    flat = f_ref[...]
    for g in range(pn.groups):
        for kv in range(2):
            w = wkv_ref[:, kv * qw + g * gw : kv * qw + (g + 1) * gw]
            got = jnp.dot(flat, w, preferred_element_type=F32)
            got = got.reshape(pn.rows, pn.cols // OCT, OCT, gw)
            for o in range(1, pn.octets - 1):
                ext[g, pl.ds(pn.own_at(o), pn.half), kv * gw : (kv + 1) * gw] = (
                    got[:, o - 1].reshape(pn.half, gw).astype(BF16)
                )
        for i in range(nreg):
            halo(g, i).start()

    if pn.group_all:
        slot = dp * 4 + lat
        fall[slot] = flat

        def flip(kind):
            return ((1 - dp, lat, lon), (dp, lax.rem(lat + 2, 4), lon), (dp, lat + 1 - 2 * lax.rem(lat, 2), lon))[kind]

        def slot_of(ddp, dx):
            return (dp + ddp - 2 * dp * ddp) * 4 + lax.rem(lat + 2 * dx, 4)

        hops = [(0, 0, 0), (1, 0, 0), (2, 0, 0), (1, 1, 0), (2, 1, 0), (2, 0, 1), (2, 1, 1)]

        def hop(n):
            kind, ddp, dx = hops[n]
            s = slot_of(ddp, dx)
            return remote(fall.at[s], fall.at[s], fs.at[n], fr.at[n], flip(kind))

        def hop_in(n):
            kind, ddp, dx = hops[n]
            if kind == 0:
                s = slot_of(1 - ddp, dx)
            elif kind == 1:
                s = slot_of(ddp, 1 - dx)
            else:
                mate = lat + 1 - 2 * lax.rem(lat, 2)
                s = (dp + ddp - 2 * dp * ddp) * 4 + lax.rem(mate + 2 * dx, 4)
            return remote(fall.at[s], fall.at[s], fs.at[n], fr.at[n], flip(kind))

        for n in (0, 1, 2):
            hop(n).start()

    lane = lax.broadcasted_iota(jnp.int32, (pn.nq, gw), 1)
    for g in range(pn.groups):
        got = jnp.dot(flat, wq_ref[:, g * gw : (g + 1) * gw], preferred_element_type=F32)
        dout = d_ref[:, g * gw : (g + 1) * gw].astype(F32)
        for hh in range(2):
            mine = (lane < hd) if hh == 0 else (lane >= hd)
            q2[g, hh * pn.nq : (hh + 1) * pn.nq] = jnp.where(mine, got, 0.0).astype(BF16)
            do2[g, hh * pn.nq : (hh + 1) * pn.nq] = jnp.where(mine, dout, 0.0).astype(BF16)

    nlat_all, nlon_all = valid_ref.shape

    def parts_of(n):
        shape = (pn.octets, pn.ext, OCT, n)
        o, row, c = (lax.broadcasted_iota(jnp.int32, shape, k).reshape(pn.nk, n) for k in range(3))
        return o * OCT + c, row, lax.broadcasted_iota(jnp.int32, (pn.nk, n), 1)

    col, row, li = parts_of(nlat_all)
    pick_row = jnp.where(li == row - pn.reach + lat * pn.rows, 1.0, 0.0).astype(BF16)
    col, row, li = parts_of(nlon_all)
    here = col - OCT + lon * pn.cols
    here = jnp.where(here < 0, here + nlon_all, here)
    here = jnp.where(here >= nlon_all, here - nlon_all, here)
    pick_col = li == here
    ones = jnp.ones((nlon_all, pn.nq), BF16)

    def key_values(ref):
        rows_of = jnp.dot(pick_row, ref[...].astype(F32).astype(BF16), preferred_element_type=F32)
        return jnp.dot(jnp.where(pick_col, rows_of, 0.0).astype(BF16), ones, preferred_element_type=F32)

    land = key_values(land_ref)
    ok = key_values(valid_ref)
    col, row, li = parts_of(pn.nq)
    a = row - li // pn.cols
    b = col - OCT + pn.reach - li % pn.cols
    side = 2 * pn.reach
    inside = (a >= 0) & (a <= side) & (b >= 0) & (b <= side)
    centre = (a == pn.reach) & (b == pn.reach)
    okay[...] = jnp.where(inside, jnp.where(centre, 1.0, ok), 0.0)
    per = pn.nq // pn.cols
    for g in range(pn.groups):
        for hh in range(2):
            h = 2 * g + hh
            for o in range(pn.octets):
                line = lines_ref[h, o]
                width = line.shape[1]
                for k in range(min(per, pn.ext)):
                    turned = line if k == 0 else pltpu.roll(line, width - k * pn.cols, 1)
                    for m in range((pn.ext - 1) // per + 1):
                        r = pn.ext - 1 - (m * per + k)
                        if r < 0:
                            continue
                        first = (o * pn.ext + r) * OCT
                        bias[g, first : first + OCT, hh * pn.nq : (hh + 1) * pn.nq] = (
                            turned[:, m * pn.nq : (m + 1) * pn.nq]
                            + land_bias_ref[h] * land[first : first + OCT]
                        )

    def step(g, carry):
        for i in range(nreg):
            halo(g, i).wait_recv()
        key = ext[g, :, 0:gw]
        value = ext[g, :, gw : 2 * gw]
        qg, dg = q2[g], do2[g]
        raw = lax.dot_general(key, qg, NEAR, preferred_element_type=F32) * scale + bias[g]
        dots = lax.dot_general(value, dg, NEAR, preferred_element_type=F32)
        bent = jnp.tanh(raw * (1.0 / CAP))
        ok1 = okay[...]
        expd = jnp.exp(CAP * bent) * jnp.concatenate([ok1, ok1], axis=1)
        weight = expd * (1.0 / jnp.sum(expd, axis=0, keepdims=True))
        delta = jnp.sum(weight * dots, axis=0, keepdims=True)
        ds = (weight * (dots - delta) * ((1.0 - bent * bent) * scale)).astype(BF16)
        wb = weight.astype(BF16)
        for kv, (left, right) in enumerate(((ds, qg), (wb, dg))):
            got = jnp.dot(left, right, preferred_element_type=F32)
            for o in range(1, pn.octets - 1):
                own[g, pl.ds((o - 1) * pn.half, pn.half), kv * gw : (kv + 1) * gw] = got[
                    pn.own_at(o) : pn.own_at(o) + pn.half
                ]
            gsend[g, :, kv * gw : (kv + 1) * gw] = got.astype(BF16)
        for i in range(nreg):
            back(g, i).start()
        turned = lax.dot_general(key, ds, TALL, preferred_element_type=F32)
        both = jnp.concatenate([turned[:hd, : pn.nq], turned[hd:, pn.nq :]], axis=0)
        dq_s[g] = both.T.astype(BF16)
        return carry

    if pn.group_all:
        lax.fori_loop(0, 1, step, 0)
        hop_in(0).wait_recv()
        hop(3).start()
        hop(4).start()
        lax.fori_loop(1, pn.groups - 1, step, 0)
        hop_in(1).wait_recv()
        hop(5).start()
        hop_in(3).wait_recv()
        hop(6).start()
        lax.fori_loop(pn.groups - 1, pn.groups, step, 0)
    else:
        lax.fori_loop(0, pn.groups, step, 0)

    dq = jnp.concatenate([dq_s[g] for g in range(pn.groups)], axis=1)
    first = lax.dot_general(dq, wq_ref[...], NEAR, preferred_element_type=F32)
    if pn.group_all:
        fsum[...] = first

        def kcopy(n, out):
            d, x = n // 4, n % 4
            tdp = lax.rem(dp + d, 2)
            tlat = lax.rem(lat + x, 4)
            fdp = lax.rem(dp + d, 2)
            flat_ = lax.rem(lat + 4 - x, 4)
            to = tdp * 4 + tlat
            frm = slot if out else fdp * 4 + flat_
            return remote(
                cell.at[to], kall.at[frm], ks.at[n], kr.at[n], (tdp, tlat, lon)
            )

        target = cell
    nat = pn.cols // OCT
    pieces = {}
    for g in range(pn.groups):
        for i in range(nreg):
            back(g, i).wait_recv()
        halves = []
        for o in range(1, pn.octets - 1):
            total = own[g, pl.ds((o - 1) * pn.half, pn.half)]
            for step_, part, owner, start, count, where in pn.regions:
                if owner != o:
                    continue
                add = grecv[g, pl.ds(where, count)].astype(F32)
                if count < pn.half:
                    zero = jnp.zeros((pn.half - count, add.shape[1]), F32)
                    add = jnp.concatenate([zero, add] if start else [add, zero], axis=0)
                total = total + add
            halves.append(total.reshape(pn.rows, 1, OCT, 2 * gw))
        full = jnp.concatenate(halves, axis=1).reshape(pn.nq, 2 * gw).astype(BF16)
        for kv in range(2):
            pieces[kv * pn.groups + g] = full[:, kv * gw : (kv + 1) * gw]
            if pn.group_all:
                cell[kv * pn.groups + g] = full[:, kv * gw : (kv + 1) * gw]
    if pn.group_all:
        for n in range(1, 8):
            kcopy(n, True).start()
    cells = jnp.concatenate([pieces[k] for k in range(2 * pn.groups)], axis=1)
    second = lax.dot_general(cells, wkv_ref[...], NEAR, preferred_element_type=F32)
    if not pn.group_all:
        cell_out[...] = cells
        fg_out[...] = (first + second).astype(BF16)
    else:
        fg_out[...] = (fsum[...] + second).astype(BF16)
        kall[slot] = cell[slot]
        for n in (2, 4, 5, 6):
            hop_in(n).wait_recv()
        for n in range(1, 8):
            kcopy(n, False).wait_recv()
        ka = kall[...].reshape(8 * pn.nq, gw)
        fa = fall[...].reshape(8 * pn.nq, fall.shape[2])
        grad = lax.dot_general(ka, fa, TALL, preferred_element_type=F32).T
        depth = grad.shape[0] // (8 * nlon)
        grad = (grad * norm).reshape(8, nlon, depth, gw)

        def zcopy(n):
            to = lax.rem(lon + n, nlon)
            return remote(zsend.at[to], zrecv.at[n - 1], zs.at[n - 1], zr.at[n - 1], (dp, lat, to))

        for z in range(nlon):
            zsend[z] = grad[:, z].reshape(8 * depth, gw).astype(BF16)
        for n in range(1, nlon):
            zcopy(n).start()
        for n in range(1, nlon):
            zcopy(n).wait_recv()
        total = zsend[lon].astype(F32)
        for n in range(1, nlon):
            total = total + zrecv[n - 1].astype(F32)
        ocol[...] = total.reshape(8, depth, gw)

        def ocopy(n, out):
            d, x = n // 4, n % 4
            tdp = lax.rem(dp + d, 2)
            tlat = lax.rem(lat + x, 4)
            frm = slot if out else tdp * 4 + lax.rem(lat + 4 - x, 4)
            where = pl.ds(pl.multiple_of(frm * gw, gw), gw)
            return remote(
                ocol.at[tdp * 4 + tlat], kv_out.at[:, where], os_.at[n], or_.at[n], (tdp, tlat, lon)
            )

        for n in range(1, 8):
            ocopy(n, True).start()
        kv_out[:, pl.ds(pl.multiple_of(slot * gw, gw), gw)] = ocol[slot]
        for n in range(1, 8):
            ocopy(n, False).wait_recv()
        for n in range(1, 8):
            kcopy(n, True).wait_send()
            ocopy(n, True).wait_send()
        for n in range(1, nlon):
            zcopy(n).wait_send()
        for n in range(7):
            hop(n).wait_send()
    for g in range(pn.groups):
        for i in range(nreg):
            halo(g, i).wait_send()
            back(g, i).wait_send()


def bias_lines(position_bias, pn):
    heads, side, _ = position_bias.shape
    lanes = 4 * pn.nq
    turns = lanes // pn.cols
    turned = jnp.flip(position_bias, axis=1)
    before = pn.ext - side
    turned = jnp.pad(turned, ((0, 0), (before, turns - before - side), (0, 0)))
    keys = pn.octets * OCT
    k = jnp.arange(keys)[None, :, None]
    c = jnp.arange(pn.cols)[None, None, :]
    hot = (jnp.arange(side)[:, None, None] == k - c + pn.reach - OCT).astype(F32)
    lines = jnp.einsum("htb,bkc->hktc", turned, hot, precision=lax.Precision.HIGHEST)
    return lines.reshape(heads, pn.octets, OCT, lanes)


def shards(
    fields, cotangent, query_weight, keyval_weight, position_bias, land_bias, valid_cell, land_sea
):
    rows, cols, width = fields.shape[1:]
    q_width = query_weight.shape[1]
    heads = position_bias.shape[0]
    size = q_width // heads
    reach = (position_bias.shape[1] - 1) // 2
    nlat, nlon, ndp = lax.axis_size("lat"), lax.axis_size("lon"), lax.axis_size("dp")
    pn = Plan(rows, cols, reach, heads, size, nlat, nlon, ndp)
    flat = fields.reshape(pn.nq, width)
    dout = cotangent.reshape(pn.nq, q_width)
    devices = nlat * nlon * ndp
    norm = float(pn.nq * devices) ** (-0.5)
    gw = 2 * size
    vm = pl.BlockSpec(memory_space=pltpu.VMEM)
    dma = pltpu.SemaphoreType.DMA
    nreg = len(pn.regions)
    g = pn.groups
    scratch = [
        pltpu.VMEM((g, pn.nk, 2 * gw), BF16),
        pltpu.VMEM((g, pn.nk, 2 * gw), BF16),
        pltpu.VMEM((g, pn.nk, 2 * gw), BF16),
        pltpu.VMEM((g, pn.nq, 2 * gw), F32),
        pltpu.VMEM((g, 2 * pn.nq, gw), BF16),
        pltpu.VMEM((g, 2 * pn.nq, gw), BF16),
        pltpu.VMEM((g, pn.nk, 2 * pn.nq), F32),
        pltpu.VMEM((pn.nk, pn.nq), F32),
        pltpu.VMEM((g, pn.nq, gw), BF16),
        dma((g, nreg)), dma((g, nreg)), dma((g, nreg)), dma((g, nreg)),
    ]
    out_shape = [jax.ShapeDtypeStruct((pn.nq, width), BF16)]
    if pn.group_all:
        depth = width // devices
        out_shape.append(jax.ShapeDtypeStruct((depth, 2 * q_width), F32))
        scratch += [
            pltpu.VMEM((8, pn.nq, width), BF16),
            pltpu.VMEM((8, pn.nq, gw), BF16),
            pltpu.VMEM((8, pn.nq, gw), BF16),
            pltpu.VMEM((nlon, 8 * depth, gw), BF16),
            pltpu.VMEM((nlon - 1, 8 * depth, gw), BF16),
            pltpu.VMEM((pn.nq, width), F32),
            pltpu.VMEM((8, depth, gw), F32),
            dma((7,)), dma((7,)), dma((8,)), dma((8,)),
            dma((nlon - 1,)), dma((nlon - 1,)), dma((8,)), dma((8,)),
        ]
    else:
        out_shape.append(jax.ShapeDtypeStruct((pn.nq, 2 * q_width), BF16))

    def kernel(*refs):
        body(pn, size ** (-0.5), norm, refs)

    field_grad, other = pl.pallas_call(
        kernel,
        out_shape=out_shape,
        in_specs=[vm] * 5 + [pl.BlockSpec(memory_space=pltpu.SMEM)] + [vm] * 2,
        out_specs=[vm, vm],
        scratch_shapes=scratch,
        name="attention_grads",
        compiler_params=pltpu.CompilerParams(
            collective_id=0, has_side_effects=True, vmem_limit_bytes=48 * 1024 * 1024
        ),
    )(
        flat, dout, query_weight, keyval_weight, bias_lines(position_bias, pn), land_bias,
        valid_cell, land_sea,
    )
    field_grad = field_grad.reshape(1, rows, cols, width)
    if pn.group_all:
        return field_grad, other
    term = lax.dot_general(flat, other, (((0,), (0,)), ((), ())), preferred_element_type=F32)
    keyval_grad = lax.psum_scatter(
        term * norm, ("dp", "lat", "lon"), scatter_dimension=0, tiled=True
    )
    return field_grad, keyval_grad


def solution(mesh):
    block = P("dp", "lat", "lon", None)
    in_specs = (block, block, P(), P(), P(), P(), P(), P())
    out_specs = (block, P(("dp", "lat", "lon"), None))
    return jax.shard_map(shards, mesh=mesh, in_specs=in_specs, out_specs=out_specs, check_vma=False)
```

time: 299 us -> 68.1 us (0.23)
  waiting for transfers between devices: 157 us -> 0 us
  local copies, waits for them, and re-layouts: 67.4 us -> 11.1 us
  Pallas kernels: 0 us -> 55 us
  matrix products: 35.5 us -> 1.06 us
  between operations: 14.5 us -> 0.74 us
  starting transfers between devices: 13.7 us -> 0 us
  other arithmetic: 10.1 us -> 0.01 us
    unnamed x2 -> x0, waiting for transfers between devices: 142 us -> none
    pallas_call x0 -> x1, Pallas kernels: none -> 55 us  [shards(): pl.pallas_call(kernel, out_shape=out_shape, in_specs=[vm] * 5 + [pl.Block...]
    dot_general x12 -> x1, matrix products: 35.5 us -> 1.06 us  [bias_lines(): jnp.einsum('htb,bkc->hktc', turned, hot, precision=lax.Precision.HIGHEST)]
    ppermute x8 -> x0, waiting for transfers between devices: 14.8 us -> none  [the longest x4 8.45 us: extended(): before = lax.ppermute(last, axis, up)]
    ppermute x8 -> x0, starting transfers between devices: 13.6 us -> none  [the longest x4 9.42 us: extended(): after = lax.ppermute(initial, axis, down)]
    transpose x3 -> x1, local copies, waits for them, and re-layouts: 15.7 us -> 2.76 us  [bias_lines(): jnp.einsum('htb,bkc->hktc', turned, hot, precision=lax.Precision.HIGHEST)]
    unnamed x56 -> x17, local copies, waits for them, and re-layouts: 15.5 us -> 3.55 us
    reshape x3 -> x1, local copies, waits for them, and re-layouts: 13.9 us -> 4.68 us  [bias_lines(): return lines.reshape(heads, pn.octets, OCT, lanes)]
  transfers between devices with their start and end apart: 9 -> 0, of which waited for: 4 -> 0; matrix products, arithmetic and copies ran while one was open for 17% -> 0% of each run, Pallas kernels for 0% -> 0%
where the time goes in v1:
time: 68.1 us; the launch traced here: 67.8 us
  Pallas kernels  55 us (81%)
  local copies, waits for them, and re-layouts  11.1 us (16%)
  matrix products  1.06 us (2%)
  between operations  0.74 us (1%)
    pallas_call x1, Pallas kernels, shards(): pl.pallas_call(kernel, out_shape=out_shape, in_specs=[vm] * 5 + [pl.Block...  55 us
    reshape x1, local copies, waits for them, and re-layouts, bias_lines(): return lines.reshape(heads, pn.octets, OCT, lanes)  4.68 us
    unnamed x17, local copies, waits for them, and re-layouts  3.55 us
    transpose x1, local copies, waits for them, and re-layouts, bias_lines(): jnp.einsum('htb,bkc->hktc', turned, hot, precision=lax.Precision.HIGHEST)  2.76 us

profile of v1, /device:TPU:0, one launch (start us, length us, event | category | flops | bytes accessed | tf_op | source)
XLA Modules:
  0.0 67.8 jit_solution(10221988529407399207)
XLA Ops:
  0.6 0.9 %copy.12 = f32[8,13,13]{1,2,0:T(8,128)S(1)} copy(f32[8,13,13]{2,0,1:T(8,128)} %param.12) | data formatting | bytes 10816 | tf_op args[4]
  1.6 0.1 rev.4
  1.7 1.1 %convolution_bitcast_fusion = f32[8,32,32,16]{2,1,0,3:T(8,128)S(1)} fusion(f32[8,13,13]{1,2,0:T(8,128)S(1)} %rev.4, s32[32,16]{0,1:T(8,128)S(1)} %subtract_add_fusion), kind=kOutput, calls=%fused_computation | convolution fusion | flops 20453888 | bytes 531744 | tf_op jit(solution)/shard_map/htb,bkc->hktc/dot_general | solution.py:365
  2.7 2.8 %copy.13 = f32[8,32,32,16]{3,2,1,0:T(8,128)} copy(f32[8,32,32,16]{2,1,0,3:T(8,128)S(1)} %convolution_bitcast_fusion) | data formatting | bytes 1048576 | tf_op jit(solution)/shard_map/htb,bkc->hktc/transpose | solution.py:365
  5.5 0.0 copy-start
  5.5 0.0 copy-start.2
  5.5 0.0 copy-start.3
  5.5 0.0 copy-start.4
  5.5 0.0 copy-start.5
  5.5 0.0 copy-start.6
  5.5 4.7 %reshape.36.refs_4_ = f32[8,4,8,512]{3,2,1,0:T(8,128)S(1)} reshape(f32[8,32,32,16]{3,2,1,0:T(8,128)} %copy.13) | data formatting | bytes 1048576 | tf_op jit(solution)/shard_map/reshape | solution.py:366
  10.2 0.0 copy-done
  10.2 0.0 copy-done.2
  10.2 0.0 copy-done.3
  10.2 0.0 copy-done.4
  10.2 0.0 copy-done.5
  10.3 0.0 copy-done.6
  10.3 0.0 copy-start.1
  10.3 1.2 %copy-done.1 = bf16[1024,512]{1,0:T(8,128)(2,1)S(1)} copy-done((bf16[1024,512]{1,0:T(8,128)(2,1)S(1)}, bf16[1024,512]{1,0:T(8,128)(2,1)}, u32[]{:S(2)}) %copy-start.1) | copy-done | bytes 1048600
  11.5 55.0 %attention_grads.1 = (bf16[128,1024]{1,0:T(8,128)(2,1)S(1)}, f32[32,1024]{1,0:T(8,128)S(1)}) custom-call(bf16[128,1024]{1,0:T(8,128)(2,1)S(1)} %bitcast.15, bf16[128,512]{1,0:T(8,128)(2,1)S(1)} %bitcast.17, bf16[1024,512]{1,0:T(8,128)(2,1)S(1)} %copy-done.1, bf16[1024,1024]{1,0:T(8,128)(2,1)S(1)} %copy-done, f32[8,4,8,512]{3,2,1,0:T(8,128)S(1)} %reshape.36.refs_4_, ...), custom_call_target="tpu_custom_call" | custom-call | tf_op jit(solution)/shard_map/attention_grads/pallas_call | solution.py:421
  66.5 0.7 %copy.17 = bf16[1,8,16,1024]{3,2,1,0:T(8,128)(2,1)} copy(bf16[1,8,16,1024]{3,2,1,0:T(8,128)(2,1)S(1)} %bitcast.16) | data formatting | bytes 524288
  67.2 0.7 copy.18
  (1 shorter events, 0.0 us)
Async XLA Ops:
  5.5 4.7 %copy-start = (bf16[1024,1024]{1,0:T(8,128)(2,1)S(1)}, bf16[1024,1024]{1,0:T(8,128)(2,1)}, u32[]{:S(2)}) copy-start(bf16[1024,1024]{1,0:T(8,128)(2,1)} %refs_3_.1) | copy-start | bytes 6291460
  5.5 4.7 %copy-start.2 = (bf16[1,8,16,1024]{3,2,1,0:T(8,128)(2,1)S(1)}, bf16[1,8,16,1024]{3,2,1,0:T(8,128)(2,1)}, u32[]{:S(2)}) copy-start(bf16[1,8,16,1024]{3,2,1,0:T(8,128)(2,1)} %param.8) | copy-start | bytes 786436
  5.5 4.7 %copy-start.3 = (bf16[1,8,16,512]{3,2,1,0:T(8,128)(2,1)S(1)}, bf16[1,8,16,512]{3,2,1,0:T(8,128)(2,1)}, u32[]{:S(2)}) copy-start(bf16[1,8,16,512]{3,2,1,0:T(8,128)(2,1)} %param.9) | copy-start | bytes 393220
  5.5 4.7 %copy-start.4 = (s32[32,64]{1,0:T(8,128)S(1)}, s32[32,64]{1,0:T(8,128)}, u32[]{:S(2)}) copy-start(s32[32,64]{1,0:T(8,128)} %refs_6_.1) | copy-start | bytes 24580
  5.5 4.7 %copy-start.5 = (s32[32,64]{1,0:T(8,128)S(1)}, s32[32,64]{1,0:T(8,128)}, u32[]{:S(2)}) copy-start(s32[32,64]{1,0:T(8,128)} %refs_7_.1) | copy-start | bytes 24580
  5.5 4.7 %copy-start.6 = (f32[8]{0:T(128)S(1)}, f32[8]{0:T(128)}, u32[]{:S(2)}) copy-start(f32[8]{0:T(128)} %refs_5_.1) | copy-start | bytes 100
  10.3 1.2 %copy-start.1 = (bf16[1024,512]{1,0:T(8,128)(2,1)S(1)}, bf16[1024,512]{1,0:T(8,128)(2,1)}, u32[]{:S(2)}) copy-start(bf16[1024,512]{1,0:T(8,128)(2,1)} %refs_2_.1) | copy-start | bytes 3145732

commit v2 on v1

--- a/solution.py
+++ b/solution.py
@@ -29,14 +29,18 @@
         last = self.octets - 1
         for o in range(self.octets):
             for part in (-1, 0, 1):
-                step = -1 if o == 0 else (1 if o == last else 0)
+                step = (-1 if o == 0 else (1 if o == last else 0)) if part == 0 else 0
                 if step == 0 and part == 0:
                     continue
-                owner = last - 1 if o == 0 else (1 if o == last else o)
+                owner = (last - 1 if o == 0 else 1) if part == 0 else o
                 start = (self.half - self.edge) if part == -1 else 0
                 count = self.half if part == 0 else self.edge
                 at = o * self.per_oct + (0 if part == -1 else self.edge + (0 if part == 0 else self.half))
                 self.regions.append((step, part, owner, start, count, at))
+        self.lon_ids = [i for i, r in enumerate(self.regions) if r[1] == 0]
+        self.near_ids = [i for i, r in enumerate(self.regions) if r[1] and 0 < r[2] < last]
+        self.corner_ids = [i for i, r in enumerate(self.regions) if r[1] and r[2] in (0, last)]
+        self.lat_ids = self.near_ids + self.corner_ids
         self.group_all = dp == 2 and lat == 4
 
     def own_at(self, o):
@@ -67,7 +71,7 @@
             lax.rem(lon + dlon + nlon, nlon) if dlon else lon,
         )
 
-    peers = [(0, a, b) for a in (-1, 0, 1) for b in (-1, 0, 1) if a or b]
+    peers = [(0, a, b) for a in (-1, 0, 1) for b in (-1, 0, 1) if (a == 0) != (b == 0)]
     if pn.group_all:
         steps = [(d, a, 0) for d in range(2) for a in range(-1, 3) if d or a]
         steps += [(0, 0, b) for b in range(1, nlon)]
@@ -101,7 +105,34 @@
             gs.at[g, i], gr.at[g, i], at(part, step),
         )
 
-    nreg = len(pn.regions)
+    def only(cond, act):
+        if cond is None:
+            act()
+        else:
+            pl.when(cond)(act)
+
+    def below(part):
+        return None if part == 0 else (lat < nlat - 1 if part == -1 else lat > 0)
+
+    def above(part):
+        return below(-part)
+
+    def run(make, side, ids, g, what):
+        for part in (-1, 0, 1):
+            chosen = [i for i in ids if pn.regions[i][1] == part]
+            if chosen:
+                only(side(part), lambda: [getattr(make(g, i), what)() for i in chosen] and None)
+
+    for part in (-1, 1):
+        def clear(part=part):
+            for g in range(pn.groups):
+                for step, p, owner, start, count, where in pn.regions:
+                    if p == part:
+                        ext[g, pl.ds(where, count)] = jnp.zeros((count, 2 * gw), BF16)
+                    if p == -part:
+                        grecv[g, pl.ds(where, count)] = jnp.zeros((count, 2 * gw), BF16)
+
+        pl.when(lat == (0 if part == -1 else nlat - 1))(clear)
 
     flat = f_ref[...]
     for g in range(pn.groups):
@@ -113,8 +144,7 @@
                 ext[g, pl.ds(pn.own_at(o), pn.half), kv * gw : (kv + 1) * gw] = (
                     got[:, o - 1].reshape(pn.half, gw).astype(BF16)
                 )
-        for i in range(nreg):
-            halo(g, i).start()
+        run(halo, below, pn.lon_ids + pn.near_ids, g, "start")
 
     if pn.group_all:
         slot = dp * 4 + lat
@@ -186,12 +216,24 @@
     centre = (a == pn.reach) & (b == pn.reach)
     okay[...] = jnp.where(inside, jnp.where(centre, 1.0, ok), 0.0)
     per = pn.nq // pn.cols
+    keys, width = pn.octets * OCT, 4 * pn.nq
+    ar = lax.broadcasted_iota(jnp.int32, (16, width), 0)
+    tr = lax.broadcasted_iota(jnp.int32, (16, width), 1) // pn.cols
+    hot = jnp.where(ar == pn.ext - 1 - tr, 1.0, 0.0)
+    spread = jnp.dot(lines_ref[...], hot, precision=lax.Precision.HIGHEST, preferred_element_type=F32)
+    turn = lax.broadcasted_iota(jnp.int32, (keys, width), 1) % pn.cols
     for g in range(pn.groups):
+        run(halo, above, pn.lon_ids, g, "wait_recv")
+        run(halo, below, pn.corner_ids, g, "start")
         for hh in range(2):
             h = 2 * g + hh
+            shifted = spread[h * keys : (h + 1) * keys]
+            bit = 1
+            while bit < pn.cols:
+                shifted = jnp.where((turn & bit) != 0, pltpu.roll(shifted, bit, 0), shifted)
+                bit *= 2
             for o in range(pn.octets):
-                line = lines_ref[h, o]
-                width = line.shape[1]
+                line = shifted[o * OCT : (o + 1) * OCT]
                 for k in range(min(per, pn.ext)):
                     turned = line if k == 0 else pltpu.roll(line, width - k * pn.cols, 1)
                     for m in range((pn.ext - 1) // per + 1):
@@ -205,8 +247,7 @@
                         )
 
     def step(g, carry):
-        for i in range(nreg):
-            halo(g, i).wait_recv()
+        run(halo, above, pn.lat_ids, g, "wait_recv")
         key = ext[g, :, 0:gw]
         value = ext[g, :, gw : 2 * gw]
         qg, dg = q2[g], do2[g]
@@ -221,34 +262,58 @@
         wb = weight.astype(BF16)
         for kv, (left, right) in enumerate(((ds, qg), (wb, dg))):
             got = jnp.dot(left, right, preferred_element_type=F32)
-            for o in range(1, pn.octets - 1):
-                own[g, pl.ds((o - 1) * pn.half, pn.half), kv * gw : (kv + 1) * gw] = got[
+            for o in range(pn.octets):
+                own[g, pl.ds(o * pn.half, pn.half), kv * gw : (kv + 1) * gw] = got[
                     pn.own_at(o) : pn.own_at(o) + pn.half
                 ]
             gsend[g, :, kv * gw : (kv + 1) * gw] = got.astype(BF16)
-        for i in range(nreg):
-            back(g, i).start()
+        run(back, above, pn.lat_ids, g, "start")
         turned = lax.dot_general(key, ds, TALL, preferred_element_type=F32)
         both = jnp.concatenate([turned[:hd, : pn.nq], turned[hd:, pn.nq :]], axis=0)
         dq_s[g] = both.T.astype(BF16)
         return carry
 
-    if pn.group_all:
-        lax.fori_loop(0, 1, step, 0)
+    def summed(g, o, parts):
+        total = own[g, pl.ds(o * pn.half, pn.half)]
+        for step_, part, owner, start, count, where in pn.regions:
+            if owner != o or part not in parts:
+                continue
+            add = grecv[g, pl.ds(where, count)].astype(F32)
+            if count < pn.half:
+                zero = jnp.zeros((pn.half - count, add.shape[1]), F32)
+                add = jnp.concatenate([zero, add] if start else [add, zero], axis=0)
+            total = total + add
+        return total
+
+    def sideways(g):
+        run(back, below, pn.lat_ids, g, "wait_recv")
+        for o in (0, pn.octets - 1):
+            gsend[g, pl.ds(pn.own_at(o), pn.half)] = summed(g, o, (-1, 1)).astype(BF16)
+        run(back, below, pn.lon_ids, g, "start")
+
+    def later(g, carry):
+        step(g, carry)
+        sideways(g - 1)
+        return carry
+
+    if pn.group_all:
+        step(0, 0)
         hop_in(0).wait_recv()
         hop(3).start()
         hop(4).start()
-        lax.fori_loop(1, pn.groups - 1, step, 0)
+        lax.fori_loop(1, pn.groups - 1, later, 0)
         hop_in(1).wait_recv()
         hop(5).start()
         hop_in(3).wait_recv()
         hop(6).start()
-        lax.fori_loop(pn.groups - 1, pn.groups, step, 0)
+        lax.fori_loop(pn.groups - 1, pn.groups, later, 0)
     else:
-        lax.fori_loop(0, pn.groups, step, 0)
+        step(0, 0)
+        lax.fori_loop(1, pn.groups, later, 0)
 
     dq = jnp.concatenate([dq_s[g] for g in range(pn.groups)], axis=1)
     first = lax.dot_general(dq, wq_ref[...], NEAR, preferred_element_type=F32)
+    sideways(pn.groups - 1)
     if pn.group_all:
         fsum[...] = first
 
@@ -265,22 +330,12 @@
             )
 
         target = cell
-    nat = pn.cols // OCT
     pieces = {}
     for g in range(pn.groups):
-        for i in range(nreg):
-            back(g, i).wait_recv()
+        run(back, below, pn.lon_ids, g, "wait_recv")
         halves = []
         for o in range(1, pn.octets - 1):
-            total = own[g, pl.ds((o - 1) * pn.half, pn.half)]
-            for step_, part, owner, start, count, where in pn.regions:
-                if owner != o:
-                    continue
-                add = grecv[g, pl.ds(where, count)].astype(F32)
-                if count < pn.half:
-                    zero = jnp.zeros((pn.half - count, add.shape[1]), F32)
-                    add = jnp.concatenate([zero, add] if start else [add, zero], axis=0)
-                total = total + add
+            total = summed(g, o, (-1, 0, 1))
             halves.append(total.reshape(pn.rows, 1, OCT, 2 * gw))
         full = jnp.concatenate(halves, axis=1).reshape(pn.nq, 2 * gw).astype(BF16)
         for kv in range(2):
@@ -346,24 +401,17 @@
         for n in range(7):
             hop(n).wait_send()
     for g in range(pn.groups):
-        for i in range(nreg):
-            halo(g, i).wait_send()
-            back(g, i).wait_send()
-
-
-def bias_lines(position_bias, pn):
+        run(halo, below, pn.lon_ids + pn.lat_ids, g, "wait_send")
+        run(back, above, pn.lat_ids, g, "wait_send")
+        run(back, above, pn.lon_ids, g, "wait_send")
+
+
+def padded_bias(position_bias, pn):
     heads, side, _ = position_bias.shape
-    lanes = 4 * pn.nq
-    turns = lanes // pn.cols
-    turned = jnp.flip(position_bias, axis=1)
-    before = pn.ext - side
-    turned = jnp.pad(turned, ((0, 0), (before, turns - before - side), (0, 0)))
-    keys = pn.octets * OCT
-    k = jnp.arange(keys)[None, :, None]
-    c = jnp.arange(pn.cols)[None, None, :]
-    hot = (jnp.arange(side)[:, None, None] == k - c + pn.reach - OCT).astype(F32)
-    lines = jnp.einsum("htb,bkc->hktc", turned, hot, precision=lax.Precision.HIGHEST)
-    return lines.reshape(heads, pn.octets, OCT, lanes)
+    lead, keys = OCT - pn.reach, pn.octets * OCT
+    turned = jnp.swapaxes(position_bias, 1, 2)
+    turned = jnp.pad(turned, ((0, 0), (lead, keys - side - lead), (0, 16 - side)))
+    return turned.reshape(heads * keys, 16)
 
 
 def shards(
@@ -389,7 +437,7 @@
         pltpu.VMEM((g, pn.nk, 2 * gw), BF16),
         pltpu.VMEM((g, pn.nk, 2 * gw), BF16),
         pltpu.VMEM((g, pn.nk, 2 * gw), BF16),
-        pltpu.VMEM((g, pn.nq, 2 * gw), F32),
+        pltpu.VMEM((g, pn.octets * pn.half, 2 * gw), F32),
         pltpu.VMEM((g, 2 * pn.nq, gw), BF16),
         pltpu.VMEM((g, 2 * pn.nq, gw), BF16),
         pltpu.VMEM((g, pn.nk, 2 * pn.nq), F32),
@@ -429,7 +477,7 @@
             collective_id=0, has_side_effects=True, vmem_limit_bytes=48 * 1024 * 1024
         ),
     )(
-        flat, dout, query_weight, keyval_weight, bias_lines(position_bias, pn), land_bias,
+        flat, dout, query_weight, keyval_weight, padded_bias(position_bias, pn), land_bias,
         valid_cell, land_sea,
     )
     field_grad = field_grad.reshape(1, rows, cols, width)

time: 68.1 us -> 59.7 us (0.88)
  Pallas kernels: 55 us -> 49.5 us
  local copies, waits for them, and re-layouts: 11.1 us -> 9.07 us
  matrix products: 1.06 us -> 0 us
    unnamed x17, local copies, waits for them, and re-layouts: 3.55 us -> 9.05 us
    pallas_call x1, Pallas kernels: 55 us -> 49.5 us  [shards(): pl.pallas_call(kernel, out_shape=out_shape, in_specs=[vm] * 5 + [pl.Block...]
    reshape x1 -> x0, local copies, waits for them, and re-layouts: 4.68 us -> none  [bias_lines(): return lines.reshape(heads, pn.octets, OCT, lanes)]
    transpose x1 -> x0, local copies, waits for them, and re-layouts: 2.76 us -> none  [bias_lines(): jnp.einsum('htb,bkc->hktc', turned, hot, precision=lax.Precision.HIGHEST)]
    dot_general x1 -> x0, matrix products: 1.06 us -> none  [bias_lines(): jnp.einsum('htb,bkc->hktc', turned, hot, precision=lax.Precision.HIGHEST)]
where the time goes in v2:
time: 59.7 us; the launch traced here: 59.2 us
  Pallas kernels  49.5 us (83%)
  local copies, waits for them, and re-layouts  9.07 us (15%)
  between operations  0.66 us (1%)
    pallas_call x1, Pallas kernels, shards(): pl.pallas_call(kernel, out_shape=out_shape, in_specs=[vm] * 5 + [pl.Block...  49.5 us
    unnamed x17, local copies, waits for them, and re-layouts  9.05 us

profile of v2, /device:TPU:0, one launch (start us, length us, event | category | flops | bytes accessed | tf_op | source)
XLA Modules:
  0.0 59.2 jit_solution(3308522166089991882)
XLA Ops:
  0.6 0.9 %copy.11 = f32[8,13,13]{2,1,0:T(8,128)S(1)} copy(f32[8,13,13]{1,0,2:T(8,128)} %bitcast.9) | data formatting | bytes 10816
  1.6 0.0 copy-start
  1.6 1.6 %copy-done = bf16[1024,1024]{1,0:T(8,128)(2,1)S(1)} copy-done((bf16[1024,1024]{1,0:T(8,128)(2,1)S(1)}, bf16[1024,1024]{1,0:T(8,128)(2,1)}, u32[]{:S(2)}) %copy-start) | copy-done | bytes 2097176
  3.2 0.0 copy-start.1
  3.2 1.2 %copy-done.1 = bf16[1024,512]{1,0:T(8,128)(2,1)S(1)} copy-done((bf16[1024,512]{1,0:T(8,128)(2,1)S(1)}, bf16[1024,512]{1,0:T(8,128)(2,1)}, u32[]{:S(2)}) %copy-start.1) | copy-done | bytes 1048600
  4.4 0.0 copy-start.2
  4.4 0.9 %copy-done.2 = bf16[1,8,16,1024]{3,2,1,0:T(8,128)(2,1)S(1)} copy-done((bf16[1,8,16,1024]{3,2,1,0:T(8,128)(2,1)S(1)}, bf16[1,8,16,1024]{3,2,1,0:T(8,128)(2,1)}, u32[]{:S(2)}) %copy-start.2) | copy-done | bytes 262168
  5.4 0.0 copy-start.3
  5.4 0.9 %copy-done.3 = bf16[1,8,16,512]{3,2,1,0:T(8,128)(2,1)S(1)} copy-done((bf16[1,8,16,512]{3,2,1,0:T(8,128)(2,1)S(1)}, bf16[1,8,16,512]{3,2,1,0:T(8,128)(2,1)}, u32[]{:S(2)}) %copy-start.3) | copy-done | bytes 131096
  6.3 0.0 copy-start.4
  6.3 0.7 %copy-done.4 = s32[32,64]{1,0:T(8,128)S(1)} copy-done((s32[32,64]{1,0:T(8,128)S(1)}, s32[32,64]{1,0:T(8,128)}, u32[]{:S(2)}) %copy-start.4) | copy-done | bytes 8216
  7.0 0.0 copy-start.5
  7.0 0.7 %copy-done.5 = s32[32,64]{1,0:T(8,128)S(1)} copy-done((s32[32,64]{1,0:T(8,128)S(1)}, s32[32,64]{1,0:T(8,128)}, u32[]{:S(2)}) %copy-start.5) | copy-done | bytes 8216
  7.7 0.0 copy-start.6
  7.7 0.7 %copy-done.6 = f32[8]{0:T(128)S(1)} copy-done((f32[8]{0:T(128)S(1)}, f32[8]{0:T(128)}, u32[]{:S(2)}) %copy-start.6) | copy-done | bytes 56
  8.4 49.5 %attention_grads.1 = (bf16[128,1024]{1,0:T(8,128)(2,1)S(1)}, f32[32,1024]{1,0:T(8,128)S(1)}) custom-call(bf16[128,1024]{1,0:T(8,128)(2,1)S(1)} %bitcast.6, bf16[128,512]{1,0:T(8,128)(2,1)S(1)} %bitcast.8, bf16[1024,512]{1,0:T(8,128)(2,1)S(1)} %copy-done.1, bf16[1024,1024]{1,0:T(8,128)(2,1)S(1)} %copy-done, f32[256,16]{1,0:T(8,128)S(1)} %bitcast.5, ...), custom_call_target="tpu_custom_call" | custom-call | tf_op jit(solution)/shard_map/attention_grads/pallas_call | solution.py:469
  57.9 0.7 %copy.14 = bf16[1,8,16,1024]{3,2,1,0:T(8,128)(2,1)} copy(bf16[1,8,16,1024]{3,2,1,0:T(8,128)(2,1)S(1)} %bitcast.7) | data formatting | bytes 524288
  58.6 0.7 %copy.15 = f32[32,1024]{1,0:T(8,128)} copy(f32[32,1024]{1,0:T(8,128)S(1)} %get-tuple-element.9) | data formatting | bytes 262144
  (1 shorter events, 0.0 us)
Async XLA Ops:
  1.6 1.6 %copy-start = (bf16[1024,1024]{1,0:T(8,128)(2,1)S(1)}, bf16[1024,1024]{1,0:T(8,128)(2,1)}, u32[]{:S(2)}) copy-start(bf16[1024,1024]{1,0:T(8,128)(2,1)} %refs_3_.1) | copy-start | bytes 6291460
  3.2 1.2 %copy-start.1 = (bf16[1024,512]{1,0:T(8,128)(2,1)S(1)}, bf16[1024,512]{1,0:T(8,128)(2,1)}, u32[]{:S(2)}) copy-start(bf16[1024,512]{1,0:T(8,128)(2,1)} %refs_2_.1) | copy-start | bytes 3145732
  4.4 0.9 %copy-start.2 = (bf16[1,8,16,1024]{3,2,1,0:T(8,128)(2,1)S(1)}, bf16[1,8,16,1024]{3,2,1,0:T(8,128)(2,1)}, u32[]{:S(2)}) copy-start(bf16[1,8,16,1024]{3,2,1,0:T(8,128)(2,1)} %param.8) | copy-start | bytes 786436
  5.4 0.9 %copy-start.3 = (bf16[1,8,16,512]{3,2,1,0:T(8,128)(2,1)S(1)}, bf16[1,8,16,512]{3,2,1,0:T(8,128)(2,1)}, u32[]{:S(2)}) copy-start(bf16[1,8,16,512]{3,2,1,0:T(8,128)(2,1)} %param.9) | copy-start | bytes 393220
  6.3 0.7 %copy-start.4 = (s32[32,64]{1,0:T(8,128)S(1)}, s32[32,64]{1,0:T(8,128)}, u32[]{:S(2)}) copy-start(s32[32,64]{1,0:T(8,128)} %refs_6_.1) | copy-start | bytes 24580
  7.0 0.7 %copy-start.5 = (s32[32,64]{1,0:T(8,128)S(1)}, s32[32,64]{1,0:T(8,128)}, u32[]{:S(2)}) copy-start(s32[32,64]{1,0:T(8,128)} %refs_7_.1) | copy-start | bytes 24580
  7.7 0.7 %copy-start.6 = (f32[8]{0:T(128)S(1)}, f32[8]{0:T(128)}, u32[]{:S(2)}) copy-start(f32[8]{0:T(128)} %refs_5_.1) | copy-start | bytes 100

commit v3 on v2

--- a/solution.py
+++ b/solution.py
@@ -41,14 +41,14 @@
         self.near_ids = [i for i, r in enumerate(self.regions) if r[1] and 0 < r[2] < last]
         self.corner_ids = [i for i, r in enumerate(self.regions) if r[1] and r[2] in (0, last)]
         self.lat_ids = self.near_ids + self.corner_ids
-        self.group_all = dp == 2 and lat == 4
+        self.group_all = dp == 2 and lat == 4 and self.groups == 4
 
     def own_at(self, o):
         return o * self.per_oct + self.edge
 
 
 def body(pn, scale, norm, refs):
-    (f_ref, d_ref, wq_ref, wkv_ref, lines_ref, land_bias_ref, valid_ref, land_ref) = refs[:8]
+    (f_hbm, d_hbm, wq_hbm, wkv_hbm, lines_ref, land_bias_ref, valid_hbm, land_hbm) = refs[:8]
     if pn.group_all:
         fg_out, kv_out = refs[8:10]
         rest = refs[10:]
@@ -56,8 +56,9 @@
         fg_out, cell_out = refs[8:10]
         rest = refs[10:]
     (ext, gsend, grecv, own, q2, do2, bias, okay, dq_s, hs, hr, gs, gr) = rest[:13]
-    if pn.group_all:
-        (fall, cell, kall, zsend, zrecv, fsum, ocol, fs, fr, ks, kr, zs, zr, os_, or_) = rest[13:]
+    (f_ref, d_ref, wq_ref, wkv_ref, valid_ref, land_ref, cell, ins) = rest[13:21]
+    if pn.group_all:
+        (fall, kall, zsend, zrecv, fsum, ocol, fs, fr, ks, kr, zs, zr, os_, or_) = rest[21:]
     lat, lon, dp = lax.axis_index("lat"), lax.axis_index("lon"), lax.axis_index("dp")
     nlat, nlon = pn.lat, pn.lon
     hd = pn.size
@@ -79,6 +80,22 @@
             seen = {(u, v % nlat, w % nlon) for u, v, w in peers}
             if (d, a % nlat, b % nlon) not in seen:
                 peers.append((d, a, b))
+    def bring(n):
+        if n < 2 * pn.groups:
+            part = pl.ds(((n % 2) * pn.groups + n // 2) * gw, gw)
+            src, dst = wkv_hbm.at[:, part], wkv_ref.at[:, part]
+        else:
+            src, dst = (
+                (f_hbm, f_ref), (wq_hbm, wq_ref), (d_hbm, d_ref), (valid_hbm, valid_ref), (land_hbm, land_ref)
+            )[n - 2 * pn.groups]
+        return pltpu.make_async_copy(src, dst, ins.at[n])
+
+    last_in = 2 * pn.groups
+    bring(last_in).start()
+    for n in range(last_in):
+        bring(n).start()
+    for n in range(last_in + 1, last_in + 5):
+        bring(n).start()
     barrier = pltpu.get_barrier_semaphore()
     for d, a, b in peers:
         pl.semaphore_signal(barrier, inc=1, device_id=at(a, b, d), device_id_type=MESH)
@@ -134,8 +151,11 @@
 
         pl.when(lat == (0 if part == -1 else nlat - 1))(clear)
 
+    bring(last_in).wait()
     flat = f_ref[...]
     for g in range(pn.groups):
+        bring(2 * g).wait()
+        bring(2 * g + 1).wait()
         for kv in range(2):
             w = wkv_ref[:, kv * qw + g * gw : kv * qw + (g + 1) * gw]
             got = jnp.dot(flat, w, preferred_element_type=F32)
@@ -174,8 +194,10 @@
                 s = (dp + ddp - 2 * dp * ddp) * 4 + lax.rem(mate + 2 * dx, 4)
             return remote(fall.at[s], fall.at[s], fs.at[n], fr.at[n], flip(kind))
 
-        for n in (0, 1, 2):
+        for n in (0, 2):
             hop(n).start()
+    for n in range(last_in + 1, last_in + 5):
+        bring(n).wait()
 
     lane = lax.broadcasted_iota(jnp.int32, (pn.nq, gw), 1)
     for g in range(pn.groups):
@@ -291,61 +313,57 @@
             gsend[g, pl.ds(pn.own_at(o), pn.half)] = summed(g, o, (-1, 1)).astype(BF16)
         run(back, below, pn.lon_ids, g, "start")
 
+    def kcopy(g, kv):
+        to = kv * pn.groups + g
+        return remote(cell.at[to], kall.at[slot], ks.at[to], kr.at[slot], (kv, g, lon))
+
+    def kcopy_in(n):
+        frm = lax.rem(slot + n, 8)
+        return remote(cell.at[frm], kall.at[frm], ks.at[frm], kr.at[frm], (frm // 4, lax.rem(frm, 4), lon))
+
+    def finish(g):
+        run(back, below, pn.lon_ids, g, "wait_recv")
+        halves = []
+        for o in range(1, pn.octets - 1):
+            halves.append(summed(g, o, (-1, 0, 1)).reshape(pn.rows, 1, OCT, 2 * gw))
+        full = jnp.concatenate(halves, axis=1).reshape(pn.nq, 2 * gw).astype(BF16)
+        for kv in range(2):
+            cell[kv * pn.groups + g] = full[:, kv * gw : (kv + 1) * gw]
+            if pn.group_all:
+                pl.when(kv * pn.groups + g != slot)(lambda kv=kv: kcopy(g, kv).start())
+
     def later(g, carry):
         step(g, carry)
         sideways(g - 1)
         return carry
 
+    def last(g, carry):
+        later(g, carry)
+        finish(g - 2)
+        return carry
+
     if pn.group_all:
         step(0, 0)
         hop_in(0).wait_recv()
-        hop(3).start()
-        hop(4).start()
-        lax.fori_loop(1, pn.groups - 1, later, 0)
+        for n in (1, 3, 4):
+            hop(n).start()
+    else:
+        step(0, 0)
+    later(1, 0)
+    lax.fori_loop(2, pn.groups, last, 0)
+    sideways(pn.groups - 1)
+    finish(pn.groups - 2)
+
+    dq = jnp.concatenate([dq_s[g] for g in range(pn.groups)], axis=1)
+    first = lax.dot_general(dq, wq_ref[...], NEAR, preferred_element_type=F32)
+    if pn.group_all:
+        fsum[...] = first
         hop_in(1).wait_recv()
         hop(5).start()
         hop_in(3).wait_recv()
         hop(6).start()
-        lax.fori_loop(pn.groups - 1, pn.groups, later, 0)
-    else:
-        step(0, 0)
-        lax.fori_loop(1, pn.groups, later, 0)
-
-    dq = jnp.concatenate([dq_s[g] for g in range(pn.groups)], axis=1)
-    first = lax.dot_general(dq, wq_ref[...], NEAR, preferred_element_type=F32)
-    sideways(pn.groups - 1)
-    if pn.group_all:
-        fsum[...] = first
-
-        def kcopy(n, out):
-            d, x = n // 4, n % 4
-            tdp = lax.rem(dp + d, 2)
-            tlat = lax.rem(lat + x, 4)
-            fdp = lax.rem(dp + d, 2)
-            flat_ = lax.rem(lat + 4 - x, 4)
-            to = tdp * 4 + tlat
-            frm = slot if out else fdp * 4 + flat_
-            return remote(
-                cell.at[to], kall.at[frm], ks.at[n], kr.at[n], (tdp, tlat, lon)
-            )
-
-        target = cell
-    pieces = {}
-    for g in range(pn.groups):
-        run(back, below, pn.lon_ids, g, "wait_recv")
-        halves = []
-        for o in range(1, pn.octets - 1):
-            total = summed(g, o, (-1, 0, 1))
-            halves.append(total.reshape(pn.rows, 1, OCT, 2 * gw))
-        full = jnp.concatenate(halves, axis=1).reshape(pn.nq, 2 * gw).astype(BF16)
-        for kv in range(2):
-            pieces[kv * pn.groups + g] = full[:, kv * gw : (kv + 1) * gw]
-            if pn.group_all:
-                cell[kv * pn.groups + g] = full[:, kv * gw : (kv + 1) * gw]
-    if pn.group_all:
-        for n in range(1, 8):
-            kcopy(n, True).start()
-    cells = jnp.concatenate([pieces[k] for k in range(2 * pn.groups)], axis=1)
+    finish(pn.groups - 1)
+    cells = jnp.concatenate([cell[k] for k in range(2 * pn.groups)], axis=1)
     second = lax.dot_general(cells, wkv_ref[...], NEAR, preferred_element_type=F32)
     if not pn.group_all:
         cell_out[...] = cells
@@ -356,7 +374,7 @@
         for n in (2, 4, 5, 6):
             hop_in(n).wait_recv()
         for n in range(1, 8):
-            kcopy(n, False).wait_recv()
+            kcopy_in(n).wait_recv()
         ka = kall[...].reshape(8 * pn.nq, gw)
         fa = fall[...].reshape(8 * pn.nq, fall.shape[2])
         grad = lax.dot_general(ka, fa, TALL, preferred_element_type=F32).T
@@ -394,7 +412,7 @@
         for n in range(1, 8):
             ocopy(n, False).wait_recv()
         for n in range(1, 8):
-            kcopy(n, True).wait_send()
+            kcopy_in(n).wait_send()
             ocopy(n, True).wait_send()
         for n in range(1, nlon):
             zcopy(n).wait_send()
@@ -430,6 +448,7 @@
     norm = float(pn.nq * devices) ** (-0.5)
     gw = 2 * size
     vm = pl.BlockSpec(memory_space=pltpu.VMEM)
+    hbm = pl.BlockSpec(memory_space=pl.ANY)
     dma = pltpu.SemaphoreType.DMA
     nreg = len(pn.regions)
     g = pn.groups
@@ -444,6 +463,14 @@
         pltpu.VMEM((pn.nk, pn.nq), F32),
         pltpu.VMEM((g, pn.nq, gw), BF16),
         dma((g, nreg)), dma((g, nreg)), dma((g, nreg)), dma((g, nreg)),
+        pltpu.VMEM((pn.nq, width), BF16),
+        pltpu.VMEM((pn.nq, q_width), BF16),
+        pltpu.VMEM(query_weight.shape, BF16),
+        pltpu.VMEM(keyval_weight.shape, BF16),
+        pltpu.VMEM(valid_cell.shape, jnp.int32),
+        pltpu.VMEM(land_sea.shape, jnp.int32),
+        pltpu.VMEM((2 * g, pn.nq, gw), BF16),
+        dma((2 * g + 5,)),
     ]
     out_shape = [jax.ShapeDtypeStruct((pn.nq, width), BF16)]
     if pn.group_all:
@@ -451,7 +478,6 @@
         out_shape.append(jax.ShapeDtypeStruct((depth, 2 * q_width), F32))
         scratch += [
             pltpu.VMEM((8, pn.nq, width), BF16),
-            pltpu.VMEM((8, pn.nq, gw), BF16),
             pltpu.VMEM((8, pn.nq, gw), BF16),
             pltpu.VMEM((nlon, 8 * depth, gw), BF16),
             pltpu.VMEM((nlon - 1, 8 * depth, gw), BF16),
@@ -469,12 +495,12 @@
     field_grad, other = pl.pallas_call(
         kernel,
         out_shape=out_shape,
-        in_specs=[vm] * 5 + [pl.BlockSpec(memory_space=pltpu.SMEM)] + [vm] * 2,
+        in_specs=[hbm] * 4 + [vm, pl.BlockSpec(memory_space=pltpu.SMEM)] + [hbm] * 2,
         out_specs=[vm, vm],
         scratch_shapes=scratch,
         name="attention_grads",
         compiler_params=pltpu.CompilerParams(
-            collective_id=0, has_side_effects=True, vmem_limit_bytes=48 * 1024 * 1024
+            collective_id=0, has_side_effects=True, vmem_limit_bytes=60 * 1024 * 1024
         ),
     )(
         flat, dout, query_weight, keyval_weight, padded_bias(position_bias, pn), land_bias,

time: 59.7 us -> 60 us (level)
  Pallas kernels: 49.5 us -> 54.3 us
  local copies, waits for them, and re-layouts: 9.07 us -> 4.85 us
    unnamed x17 -> x3, local copies, waits for them, and re-layouts: 9.05 us -> 4.18 us
    pallas_call x1, Pallas kernels: 49.5 us -> 54.3 us  [shards(): pl.pallas_call(kernel, out_shape=out_shape, in_specs=[hbm] * 4 + [vm, pl....]
    pad x1, local copies, waits for them, and re-layouts: 0.01 us -> 0.67 us  [padded_bias(): jnp.pad(turned, ((0, 0), (lead, keys - side - lead), (0, 16 - side)))]
where the time goes in v3:
time: 60 us; the launch traced here: 59.8 us
  Pallas kernels  54.3 us (90%)
  local copies, waits for them, and re-layouts  4.85 us (8%)
  between operations  0.64 us (1%)
    pallas_call x1, Pallas kernels, shards(): pl.pallas_call(kernel, out_shape=out_shape, in_specs=[hbm] * 4 + [vm, pl....  54.3 us
    unnamed x3, local copies, waits for them, and re-layouts  4.18 us

profile of v3, /device:TPU:0, one launch (start us, length us, event | category | flops | bytes accessed | tf_op | source)
XLA Modules:
  0.0 59.8 jit_solution(42436176708447807)
XLA Ops:
  0.6 0.9 %copy.11 = f32[8,13,13]{2,1,0:T(8,128)S(1)} copy(f32[8,13,13]{1,0,2:T(8,128)} %bitcast.9) | data formatting | bytes 10816
  1.6 0.7 %pad.4.clone = f32[8,32,16]{2,1,0:T(8,128)} pad(f32[8,13,13]{2,1,0:T(8,128)S(1)} %copy.11, f32[]{:T(128)} %constant.2.clone.1), padding=0_0x2_17x0_3 | pad | bytes 21796 | tf_op jit(solution)/shard_map/jit(_pad)/pad | solution.py:431
  2.2 54.3 %attention_grads.1 = (bf16[128,1024]{1,0:T(8,128)(2,1)}, f32[32,1024]{1,0:T(8,128)}) custom-call(bf16[128,1024]{1,0:T(8,128)(2,1)} %bitcast.6, bf16[128,512]{1,0:T(8,128)(2,1)} %bitcast.8, bf16[1024,512]{1,0:T(8,128)(2,1)} %refs_2_.1, bf16[1024,1024]{1,0:T(8,128)(2,1)} %refs_3_.1, f32[256,16]{1,0:T(8,128)} %bitcast.5, f32[8]{0:T(128)} %refs_5_.1, ...), custom_call_target="tpu_custom_call" | custom-call | tf_op jit(solution)/shard_map/attention_grads/pallas_call | solution.py:495
  56.6 1.7 %copy.14 = bf16[1,8,16,1024]{3,2,1,0:T(8,128)(2,1)} copy(bf16[1,8,16,1024]{3,2,1,0:T(8,128)(2,1)} %bitcast.7) | data formatting | bytes 524288
  58.2 1.6 %copy.15 = f32[32,1024]{1,0:T(8,128)} copy(f32[32,1024]{1,0:T(8,128)} %get-tuple-element.9) | data formatting | bytes 262144

commit v4 on v3

--- a/solution.py
+++ b/solution.py
@@ -194,7 +194,7 @@
                 s = (dp + ddp - 2 * dp * ddp) * 4 + lax.rem(mate + 2 * dx, 4)
             return remote(fall.at[s], fall.at[s], fs.at[n], fr.at[n], flip(kind))
 
-        for n in (0, 2):
+        for n in (0, 1, 2):
             hop(n).start()
     for n in range(last_in + 1, last_in + 5):
         bring(n).wait()
@@ -339,20 +339,18 @@
 
     def last(g, carry):
         later(g, carry)
-        finish(g - 2)
         return carry
 
     if pn.group_all:
         step(0, 0)
         hop_in(0).wait_recv()
-        for n in (1, 3, 4):
+        for n in (3, 4):
             hop(n).start()
     else:
         step(0, 0)
     later(1, 0)
     lax.fori_loop(2, pn.groups, last, 0)
     sideways(pn.groups - 1)
-    finish(pn.groups - 2)
 
     dq = jnp.concatenate([dq_s[g] for g in range(pn.groups)], axis=1)
     first = lax.dot_general(dq, wq_ref[...], NEAR, preferred_element_type=F32)
@@ -362,7 +360,8 @@
         hop(5).start()
         hop_in(3).wait_recv()
         hop(6).start()
-    finish(pn.groups - 1)
+    for g in range(pn.groups):
+        finish(g)
     cells = jnp.concatenate([cell[k] for k in range(2 * pn.groups)], axis=1)
     second = lax.dot_general(cells, wkv_ref[...], NEAR, preferred_element_type=F32)
     if not pn.group_all:

time: 60 us -> 54 us (0.900)
  Pallas kernels: 54.3 us -> 48.3 us
    pallas_call x1, Pallas kernels: 54.3 us -> 48.3 us  [shards(): pl.pallas_call(kernel, out_shape=out_shape, in_specs=[hbm] * 4 + [vm, pl....]
where the time goes in v4:
time: 54 us; the launch traced here: 53.8 us
  Pallas kernels  48.3 us (89%)
  local copies, waits for them, and re-layouts  4.85 us (9%)
  between operations  0.64 us (1%)
    pallas_call x1, Pallas kernels, shards(): pl.pallas_call(kernel, out_shape=out_shape, in_specs=[hbm] * 4 + [vm, pl....  48.3 us
    unnamed x3, local copies, waits for them, and re-layouts  4.18 us

profile of v4, /device:TPU:0, one launch (start us, length us, event | category | flops | bytes accessed | tf_op | source)
XLA Modules:
  0.0 53.8 jit_solution(3236466971744430373)
XLA Ops:
  0.6 0.9 %copy.11 = f32[8,13,13]{2,1,0:T(8,128)S(1)} copy(f32[8,13,13]{1,0,2:T(8,128)} %bitcast.9) | data formatting | bytes 10816
  1.6 0.7 %pad.4.clone = f32[8,32,16]{2,1,0:T(8,128)} pad(f32[8,13,13]{2,1,0:T(8,128)S(1)} %copy.11, f32[]{:T(128)} %constant.2.clone.1), padding=0_0x2_17x0_3 | pad | bytes 21796 | tf_op jit(solution)/shard_map/jit(_pad)/pad | solution.py:430
  2.2 48.3 %attention_grads.1 = (bf16[128,1024]{1,0:T(8,128)(2,1)}, f32[32,1024]{1,0:T(8,128)}) custom-call(bf16[128,1024]{1,0:T(8,128)(2,1)} %bitcast.6, bf16[128,512]{1,0:T(8,128)(2,1)} %bitcast.8, bf16[1024,512]{1,0:T(8,128)(2,1)} %refs_2_.1, bf16[1024,1024]{1,0:T(8,128)(2,1)} %refs_3_.1, f32[256,16]{1,0:T(8,128)} %bitcast.5, f32[8]{0:T(128)} %refs_5_.1, ...), custom_call_target="tpu_custom_call" | custom-call | tf_op jit(solution)/shard_map/attention_grads/pallas_call | solution.py:494
  50.6 1.7 %copy.14 = bf16[1,8,16,1024]{3,2,1,0:T(8,128)(2,1)} copy(bf16[1,8,16,1024]{3,2,1,0:T(8,128)(2,1)} %bitcast.7) | data formatting | bytes 524288
  52.2 1.6 %copy.15 = f32[32,1024]{1,0:T(8,128)} copy(f32[32,1024]{1,0:T(8,128)} %get-tuple-element.9) | data formatting | bytes 262144
